TPU v7x, 32 devices: a whole 2x2x4 slice. The times are simulated.
32 devices in a mesh: ctx: 16 (over z, x, core), fsdp: 2 (over y).
Axes of the slice: x: 2, y: 2, z: 4, core: 2. Of those that a mesh axis runs over, the one named last changes fastest.
Arguments:
- tokens: bfloat16 [2, 4096, 768], P('fsdp', 'ctx'), may hold values from -6 to 6
- query_weight: bfloat16 [768, 768], P('fsdp'), may hold values from -0.21875 to 0.21875
- query_bias: bfloat16 [768], P('fsdp'), may hold values from -1.5 to 1.5
- key_weight: bfloat16 [768, 768], P('fsdp'), may hold values from -0.21875 to 0.21875
- value_weight: bfloat16 [768, 768], P('fsdp'), may hold values from -0.21875 to 0.21875
- value_bias: bfloat16 [768], P('fsdp'), may hold values from -1.5 to 1.5
- out_weight: bfloat16 [768, 768], P('fsdp'), may hold values from -1.25 to 1.25
- out_bias: bfloat16 [768], P('fsdp'), may hold values from -1.5 to 1.5
- first_gain: bfloat16 [768], P('fsdp'), may hold values from 0.5 to 1.5
- first_shift: bfloat16 [768], P('fsdp'), may hold values from -1.5 to 1.5
- inner_weight: bfloat16 [768, 3072], P('fsdp'), may hold values from -0.21875 to 0.21875
- inner_bias: bfloat16 [3072], P('fsdp'), may hold values from -1.5 to 1.5
- outer_weight: bfloat16 [3072, 768], P('fsdp'), may hold values from -0.109375 to 0.109375
- outer_bias: bfloat16 [768], P('fsdp'), may hold values from -1.5 to 1.5
- second_gain: bfloat16 [768], P('fsdp'), may hold values from 0.5 to 1.5
- second_shift: bfloat16 [768], P('fsdp'), may hold values from -1.5 to 1.5
- doc_lengths: int32 [2, 48], P('fsdp'), may hold values from 1 to 2304, 4096 in all within a row
- grad_output: bfloat16 [2, 4096, 768], P('fsdp', 'ctx'), may hold values from -6 to 6
Outputs:
- output: bfloat16 [2, 4096, 768], P('fsdp', 'ctx')
- grad_tokens: float32 [2, 4096, 768], P('fsdp', 'ctx')
- grad_query_weight: float32 [768, 768], P('fsdp')
- grad_query_bias: float32 [768], P('fsdp')
- grad_key_weight: float32 [768, 768], P('fsdp')
- grad_value_weight: float32 [768, 768], P('fsdp')
- grad_value_bias: float32 [768], P('fsdp')
- grad_out_weight: float32 [768, 768], P('fsdp')
- grad_out_bias: float32 [768], P('fsdp')
- grad_first_gain: float32 [768], P('fsdp')
- grad_first_shift: float32 [768], P('fsdp')
- grad_inner_weight: float32 [768, 3072], P('fsdp')
- grad_inner_bias: float32 [3072], P('fsdp')
- grad_outer_weight: float32 [3072, 768], P('fsdp')
- grad_outer_bias: float32 [768], P('fsdp')
- grad_second_gain: float32 [768], P('fsdp')
- grad_second_shift: float32 [768], P('fsdp')
Inputs may be any that keep to these rules, and one draw needn't show every extreme that they name: `doc_lengths`: each row holds the 48 document lengths of one sequence in order; they sum to 4096 and the longest is exactly 2304.
All inputs are finite; a program needn't handle non-finite values.
Results may differ from a plain program's by a relative error of at most 0.018.
Values may be sent and summed in bfloat16 or wider, within the bound.
No kernel may reach another device: no remote copies, remote signals or barrier semaphores. Data moves between devices by JAX's collectives and lax.ppermute only.
A program may use at most 384 MiB of HBM per device.

v0:
```python
import functools
import math

import jax
import jax.numpy as jnp
from jax import lax
from jax.experimental import pallas as pl
from jax.experimental.pallas import tpu as pltpu
from jax.sharding import PartitionSpec as P

H = 12
HD = 64
NG = 4
HG = H // NG
GW = HG * HD

eps = 1e-12
NEG = -1e30
LOG2E = 1.4426950408889634
SCALE = 1.0 / math.sqrt(HD)
bf16 = jnp.bfloat16
f32 = jnp.float32


def layer_norm(r, gain, shift):
    mean = jnp.mean(r, axis=-1, keepdims=True)
    centered = r - mean
    var = jnp.mean(centered * centered, axis=-1, keepdims=True)
    return centered * lax.rsqrt(var + eps) * gain + shift


def gelu_exact(v):
    return jax.nn.gelu(v, approximate=False)


def dot(left, right, ldim=1, rdim=0):
    return lax.dot_general(
        left, right, (((ldim,), (rdim,)), ((), ())), preferred_element_type=f32
    )


def swap(v, axis, bit):
    n = lax.axis_size(axis)
    return lax.ppermute(v, axis, [(i, i ^ bit) for i in range(n)])


def pick(v, index, axis=0):
    return lax.dynamic_index_in_dim(v, index, axis, keepdims=False)


def ordered(bit, own, other):
    return jnp.where(bit == 0, jnp.stack([own, other]), jnp.stack([other, own]))


def slot_of(t, m, g, members):
    shift = members.bit_length() - 1
    return jnp.bitwise_xor(jnp.bitwise_and(t, members - 1), m) * NG + jnp.bitwise_xor(
        jnp.right_shift(t, shift), g
    )


def fwd_kernel(members, block, scal, st_ref, en_ref, q_ref, *rest):
    kv_refs = rest[:members]
    o_ref, ob_ref, lse_ref, k_scr, v_scr = rest[members:]
    m_id, g_id = scal[0], scal[1]
    cols = NG * block
    for s in range(members):
        for h in range(HG):
            k_scr[h, s * cols : (s + 1) * cols, :] = kv_refs[s][h * HD : (h + 1) * HD, :].T
        v_scr[:, s * cols : (s + 1) * cols] = kv_refs[s][GW:, :]
    for j in range(NG):
        qs = slice(j * block, (j + 1) * block)
        start = st_ref[:, qs]
        end = en_ref[:, qs]
        qts = [q_ref[h * HD : (h + 1) * HD, qs] for h in range(HG)]

        def step(t, carry, start=start, end=end, qts=qts):
            off = pl.multiple_of(slot_of(t, m_id, g_id, members) * block, block)
            kpos = t * block + lax.broadcasted_iota(jnp.int32, (block, block), 0)
            allowed = (kpos >= start) & (kpos < end)
            out = []
            for h in range(HG):
                top, total, acc = carry[h]
                s = dot(k_scr[h, pl.ds(off, block), :], qts[h]) * (SCALE * LOG2E)
                s = jnp.where(allowed, s, NEG)
                new = jnp.maximum(top, jnp.max(s, axis=0, keepdims=True))
                alpha = jnp.exp2(top - new)
                p = jnp.exp2(s - new)
                total = total * alpha + jnp.sum(p, axis=0, keepdims=True)
                acc = acc * alpha + dot(
                    v_scr[h * HD : (h + 1) * HD, pl.ds(off, block)], p.astype(bf16)
                )
                out.append((new, total, acc))
            return tuple(out)

        init = tuple(
            (
                jnp.full((1, block), NEG, f32),
                jnp.zeros((1, block), f32),
                jnp.zeros((HD, block), f32),
            )
            for _ in range(HG)
        )
        done = lax.fori_loop(scal[2 + j], scal[2 + NG + j], step, init)
        for h in range(HG):
            top, total, acc = done[h]
            o = acc / total
            o_ref[h * HD : (h + 1) * HD, qs] = o
            ob_ref[h * HD : (h + 1) * HD, qs] = o.astype(bf16)
            lse_ref[h : h + 1, qs] = top + jnp.log2(total)


def bwd_kernel(members, block, scal, st_ref, en_ref, q_ref, o_ref, lse_ref, do_ref, *rest):
    kv_refs = rest[:members]
    dq_ref, dkv_ref, k_scr, v_scr, kt_scr, dk_scr, dv_scr = rest[members:]
    m_id, g_id = scal[0], scal[1]
    cols = NG * block
    for s in range(members):
        part = slice(s * cols, (s + 1) * cols)
        for h in range(HG):
            k_scr[h, part, :] = kv_refs[s][h * HD : (h + 1) * HD, :].T
            v_scr[h, part, :] = kv_refs[s][GW + h * HD : GW + (h + 1) * HD, :].T
        kt_scr[:, part] = kv_refs[s][:GW, :]
    dk_scr[...] = jnp.zeros_like(dk_scr)
    dv_scr[...] = jnp.zeros_like(dv_scr)
    for j in range(NG):
        qs = slice(j * block, (j + 1) * block)
        start = st_ref[:, qs]
        end = en_ref[:, qs]
        per_head = []
        for h in range(HG):
            hr = slice(h * HD, (h + 1) * HD)
            qt = q_ref[hr, qs]
            dot_t = do_ref[hr, qs]
            delta = jnp.sum(dot_t.astype(f32) * o_ref[hr, qs], axis=0, keepdims=True)
            per_head.append((qt, qt.T, dot_t, dot_t.T, delta, lse_ref[h : h + 1, qs]))

        def step(t, carry, start=start, end=end, per_head=per_head):
            off = pl.multiple_of(slot_of(t, m_id, g_id, members) * block, block)
            kpos = t * block + lax.broadcasted_iota(jnp.int32, (block, block), 0)
            allowed = (kpos >= start) & (kpos < end)
            out = []
            for h in range(HG):
                qt, q, dot_t, do, delta, lse = per_head[h]
                s = dot(k_scr[h, pl.ds(off, block), :], qt) * (SCALE * LOG2E)
                p = jnp.where(allowed, jnp.exp2(s - lse), 0.0)
                dp = dot(v_scr[h, pl.ds(off, block), :], dot_t)
                ds = (p * (dp - delta)).astype(bf16)
                dv_scr[h, pl.ds(off, block), :] += dot(p.astype(bf16), do)
                dk_scr[h, pl.ds(off, block), :] += dot(ds, q)
                out.append(
                    carry[h] + dot(kt_scr[h * HD : (h + 1) * HD, pl.ds(off, block)], ds)
                )
            return tuple(out)

        init = tuple(jnp.zeros((HD, block), f32) for _ in range(HG))
        done = lax.fori_loop(scal[2 + j], scal[2 + NG + j], step, init)
        for h in range(HG):
            dq_ref[h * HD : (h + 1) * HD, qs] = (done[h] * SCALE).astype(bf16)
    for s in range(members):
        part = slice(s * cols, (s + 1) * cols)
        for h in range(HG):
            dkv_ref[s, h * HD : (h + 1) * HD, :] = (dk_scr[h, part, :] * SCALE).T.astype(bf16)
            dkv_ref[s, GW + h * HD : GW + (h + 1) * HD, :] = dv_scr[h, part, :].T.astype(bf16)


def whole_specs(n):
    return [pl.BlockSpec(memory_space=pltpu.SMEM)] + [
        pl.BlockSpec(memory_space=pltpu.VMEM) for _ in range(n)
    ]


def attend(members, block, scal, starts, ends, q, kvs):
    keys = members * NG * block
    rows = NG * block
    return pl.pallas_call(
        functools.partial(fwd_kernel, members, block),
        out_shape=(
            jax.ShapeDtypeStruct((GW, rows), f32),
            jax.ShapeDtypeStruct((GW, rows), bf16),
            jax.ShapeDtypeStruct((HG, rows), f32),
        ),
        in_specs=whole_specs(3 + members),
        out_specs=[pl.BlockSpec(memory_space=pltpu.VMEM) for _ in range(3)],
        scratch_shapes=[
            pltpu.VMEM((HG, keys, HD), bf16),
            pltpu.VMEM((GW, keys), bf16),
        ],
        compiler_params=pltpu.CompilerParams(vmem_limit_bytes=50 << 20),
        name="attend",
    )(scal, starts, ends, q, *kvs)


def attend_back(members, block, scal, starts, ends, q, o, lse, do, kvs):
    keys = members * NG * block
    rows = NG * block
    return pl.pallas_call(
        functools.partial(bwd_kernel, members, block),
        out_shape=(
            jax.ShapeDtypeStruct((GW, rows), bf16),
            jax.ShapeDtypeStruct((members, 2 * GW, rows), bf16),
        ),
        in_specs=whole_specs(6 + members),
        out_specs=[pl.BlockSpec(memory_space=pltpu.VMEM) for _ in range(2)],
        scratch_shapes=[
            pltpu.VMEM((HG, keys, HD), bf16),
            pltpu.VMEM((HG, keys, HD), bf16),
            pltpu.VMEM((GW, keys), bf16),
            pltpu.VMEM((HG, keys, HD), f32),
            pltpu.VMEM((HG, keys, HD), f32),
        ],
        compiler_params=pltpu.CompilerParams(vmem_limit_bytes=56 << 20),
        name="attend_back",
    )(scal, starts, ends, q, o, lse, do, *kvs)


def on_device(
    tokens,
    query_weight,
    query_bias,
    key_weight,
    value_weight,
    value_bias,
    out_weight,
    out_bias,
    first_gain,
    first_shift,
    inner_weight,
    inner_bias,
    outer_weight,
    outer_bias,
    second_gain,
    second_shift,
    doc_lengths,
    grad_output,
):
    block = tokens.shape[1]
    width = tokens.shape[2]
    ctx = lax.axis_size("ctx")
    fs = lax.axis_size("fsdp")
    members = ctx // NG
    ci = lax.axis_index("ctx")
    fi = lax.axis_index("fsdp")
    g_id = ci // members
    m_id = ci % members
    core = ci % 2
    own_rows = width // fs
    m_bits = []
    b = members // 2
    while b >= 1:
        m_bits.append(b)
        b //= 2
    g_slots = range(NG)

    def bit_of(index, bit):
        return (index // bit) % 2

    def gather_rows(w):
        rows = w.shape[0]
        if fs != 2:
            return lax.all_gather(w, "fsdp", axis=0, tiled=True)
        half = rows // 2
        mine = swap(lax.dynamic_slice_in_dim(w, core * half, half, 0), "fsdp", 1)
        others = swap(mine, "ctx", 1)
        other = ordered(core, mine, others).reshape(w.shape)
        return ordered(fi, w, other).reshape((2 * rows,) + w.shape[1:])

    local = tokens[0]
    x_slots = {0: local}
    x_slots[2] = swap(local, "ctx", 2 * members)
    x_slots[1] = swap(local, "ctx", members)
    x_slots[3] = swap(x_slots[2], "ctx", members)
    x_all = jnp.concatenate([x_slots[j] for j in g_slots], axis=0)

    vectors = [
        query_bias,
        value_bias,
        out_bias,
        first_gain,
        first_shift,
        inner_bias,
        outer_bias,
        second_gain,
        second_shift,
    ]
    sizes = [v.shape[0] for v in vectors]
    packed = lax.all_gather(jnp.concatenate(vectors), "fsdp", axis=0, tiled=False)
    at = 0
    full = []
    for n in sizes:
        full.append(packed[:, at : at + n].reshape(-1).astype(f32))
        at += n
    qbias, vbias, obias, gain_one, shift_one, ibias, outbias, gain_two, shift_two = full

    group_cols = [
        lax.dynamic_slice_in_dim(w, g_id * GW, GW, 1)
        for w in (query_weight, key_weight, value_weight)
    ]
    w_group = lax.all_gather(
        jnp.concatenate(group_cols, axis=1), "fsdp", axis=0, tiled=True
    ) if fs != 2 else None
    if fs == 2:
        mine = jnp.concatenate(group_cols, axis=1)
        w_group = ordered(fi, mine, swap(mine, "fsdp", 1)).reshape(width, 3 * GW)
    out_full = gather_rows(out_weight)
    inner_full = gather_rows(inner_weight)
    outer_full = gather_rows(outer_weight)
    qkv_full = gather_rows(jnp.concatenate([query_weight, key_weight, value_weight], axis=1))

    bias_group = jnp.concatenate(
        [
            lax.dynamic_slice_in_dim(qbias, g_id * GW, GW, 0),
            jnp.zeros((GW,), f32),
            lax.dynamic_slice_in_dim(vbias, g_id * GW, GW, 0),
        ]
    )
    qkv = (dot(w_group, x_all, 0, 1) + bias_group[:, None]).astype(bf16)
    q_t = qkv[:GW]
    kv_slots = {0: qkv[GW:]}
    for b in m_bits:
        for s in sorted(kv_slots):
            kv_slots[s ^ b] = swap(kv_slots[s], "ctx", b)
    kvs = [kv_slots[s] for s in range(members)]

    doc_ends = jnp.cumsum(doc_lengths[0])
    first = jnp.stack([(jnp.bitwise_xor(g_id, j) * members + m_id) * block for j in g_slots])
    places = (first[:, None] + jnp.arange(block, dtype=jnp.int32)[None, :]).reshape(-1)
    before = places[:, None] >= doc_ends[None, :]
    starts = jnp.max(jnp.where(before, doc_ends[None, :], 0), axis=1).astype(jnp.int32)
    ends = jnp.min(jnp.where(before, ctx * block, doc_ends[None, :]), axis=1).astype(jnp.int32)
    low = starts.reshape(NG, block)[:, 0] // block
    high = (ends.reshape(NG, block)[:, -1] + block - 1) // block
    scal = jnp.concatenate([jnp.stack([m_id, g_id]), low, high]).astype(jnp.int32)
    starts = starts[None]
    ends = ends[None]

    o_t, ob_t, lse = attend(members, block, scal, starts, ends, q_t, kvs)

    def column(v, j):
        return v[:, j * block : (j + 1) * block]

    def exchange(parts):
        return [parts[0]] + [swap(parts[j], "ctx", j * members) for j in range(1, NG)]

    def by_group(slots):
        return [
            lax.select_n(g_id, *[slots[a ^ k] for k in g_slots]) for a in g_slots
        ]

    attn_t = jnp.concatenate(by_group(exchange([column(ob_t, j) for j in g_slots])), axis=0)
    branch = dot(attn_t, out_full, 0, 0) + obias
    local_float = local.astype(f32)
    hidden, first_back = jax.vjp(layer_norm, local_float + branch, gain_one, shift_one)
    hidden_low = hidden.astype(bf16)
    inner = dot(hidden_low, inner_full) + ibias
    active, gelu_back = jax.vjp(gelu_exact, inner)
    active_low = active.astype(bf16)
    outer = dot(active_low, outer_full) + outbias
    result, second_back = jax.vjp(layer_norm, hidden + outer, gain_two, shift_two)
    output = result.astype(bf16)[None]
    grad_y = grad_output[0].astype(f32)
    d_second, grad_gain_two, grad_shift_two = second_back(grad_y)
    d_outer_low = d_second.astype(bf16)
    grad_outbias = jnp.sum(d_outer_low.astype(f32), axis=0)
    (d_inner,) = gelu_back(dot(d_outer_low, outer_full, 1, 1))
    d_inner_low = d_inner.astype(bf16)
    grad_ibias = jnp.sum(d_inner_low.astype(f32), axis=0)
    d_hidden = d_second + dot(d_inner_low, inner_full, 1, 1)
    d_first, grad_gain_one, grad_shift_one = first_back(d_hidden)
    d_branch_low = d_first.astype(bf16)
    grad_obias = jnp.sum(d_branch_low.astype(f32), axis=0)
    do_t = dot(out_full, d_branch_low, 1, 1).astype(bf16).reshape(NG, GW, block)
    do_parts = [pick(do_t, jnp.bitwise_xor(g_id, j)) for j in g_slots]
    do_all = jnp.concatenate(exchange(do_parts), axis=1)

    def halve(acc, axis, bit, index):
        acc = acc.reshape((2, acc.shape[0] // 2) + acc.shape[1:])
        mine = bit_of(index, bit)
        got = swap(pick(acc, 1 - mine), axis, bit)
        return (pick(acc, mine).astype(f32) + got.astype(f32)).astype(bf16)

    def reduce_rows(product, left, bits):
        rows = left.shape[0] // (2 * fs)
        split = left.reshape(fs, 2, rows, left.shape[1])
        send = product(pick(split, 1 - core, 1).reshape(fs * rows, -1)).astype(bf16)
        keep = product(pick(split, core, 1).reshape(fs * rows, -1))
        acc = (keep + swap(send, "ctx", 1).astype(f32)).astype(bf16)
        n = fs
        while n > 1:
            n //= 2
            acc = halve(acc, "fsdp", n, fi)
        for b in bits:
            acc = halve(acc, "ctx", b, ci)
        return acc

    def join(acc, bit):
        both = ordered(bit_of(ci, bit), acc, swap(acc, "ctx", bit))
        return both.reshape((2 * acc.shape[0],) + acc.shape[1:])

    x_bits = [b for b in m_bits if b > 1]
    all_bits = x_bits + [members, 2 * members]

    def weight_grad(left_t, right, rdim=0):
        acc = reduce_rows(lambda part: dot(part, right, 1, rdim), left_t, all_bits)
        for b in all_bits[::-1]:
            acc = join(acc, b)
        return join(acc, 1).astype(f32)

    grad_outer = weight_grad(active_low.T, d_outer_low)
    grad_inner = weight_grad(hidden_low.T, d_inner_low)
    grad_out = weight_grad(attn_t, d_branch_low)

    dq_t, dkv = attend_back(members, block, scal, starts, ends, q_t, o_t, lse, do_all, kvs)
    dkv_slots = {s: dkv[s] for s in range(members)}
    for b in m_bits[::-1]:
        for s in sorted(dkv_slots):
            if s & b:
                got = swap(dkv_slots.pop(s), "ctx", b)
                dkv_slots[s ^ b] = (dkv_slots[s ^ b].astype(f32) + got.astype(f32)).astype(bf16)
    d_qkv = jnp.concatenate([dq_t, dkv_slots[0]], axis=0)
    back = by_group(exchange([column(d_qkv, j) for j in g_slots]))
    d_all = jnp.stack(back).reshape(NG, 3, GW, block).transpose(1, 0, 2, 3).reshape(3 * width, block)
    grad_input = d_first + dot(d_all, qkv_full, 0, 1)

    acc = reduce_rows(lambda part: dot(part, d_qkv, 1, 1), x_all.T, x_bits)
    acc = ordered(bit_of(ci, 2 * members), acc, swap(acc, "ctx", 2 * members))
    acc = ordered(bit_of(ci, members), acc, swap(acc, "ctx", members))
    lead = []
    for b in x_bits[::-1] + [1]:
        acc = ordered(bit_of(ci, b), acc, swap(acc, "ctx", b))
        lead.append(2)
    nb = len(lead)
    acc = acc.astype(f32)
    order = tuple(range(nb)) + (nb + 2, nb + 1, nb, nb + 3)
    acc = acc.transpose(order).reshape(own_rows, NG, 3, GW).transpose(2, 0, 1, 3)
    grad_query, grad_key, grad_value = acc.reshape(3, own_rows, width)

    group_sums = jnp.sum(d_qkv.astype(f32), axis=1)
    spread = (jnp.arange(NG) == g_id)[:, None]
    grad_qbias = jnp.where(spread, group_sums[None, :GW], 0.0).reshape(-1)
    grad_vbias = jnp.where(spread, group_sums[None, 2 * GW :], 0.0).reshape(-1)
    terms = [
        grad_qbias,
        grad_vbias,
        grad_obias,
        grad_gain_one,
        grad_shift_one,
        grad_ibias,
        grad_outbias,
        grad_gain_two,
        grad_shift_two,
    ]
    summed = lax.psum(jnp.concatenate([t.reshape(fs, -1) for t in terms], axis=1), ("fsdp", "ctx"))
    mine = pick(summed, fi)
    shares = []
    at = 0
    for n in sizes:
        shares.append(mine[at : at + n])
        at += n
    s_q, s_v, s_o, s_g1, s_s1, s_i, s_out, s_g2, s_s2 = shares
    return (
        output,
        grad_input[None],
        grad_query,
        s_q,
        grad_key,
        grad_value,
        s_v,
        grad_out,
        s_o,
        s_g1,
        s_s1,
        grad_inner,
        s_i,
        grad_outer,
        s_out,
        s_g2,
        s_s2,
    )


def vmem(n):
    return [pl.BlockSpec(memory_space=pltpu.VMEM) for _ in range(n)]


def anyspec(n):
    return [pl.BlockSpec(memory_space=pl.ANY) for _ in range(n)]


CHEAP = pl.CostEstimate(flops=1, transcendentals=0, bytes_accessed=1)
EXTRA = 8
SPARE = 64
SMEM = pl.BlockSpec(memory_space=pltpu.SMEM)


def params(mib=56):
    return pltpu.CompilerParams(vmem_limit_bytes=mib << 20)


def project_kernel(
    block, scal, x0, x1, x2, x3, own, small, small_oth, mine, sib, q_ref, kv_ref, row_scr, bias_scr, w_scr, sems
):
    g_id, fi, core = scal[0], scal[1], scal[2]
    half = own.shape[0]
    quarter = half // 2
    copies = [
        pltpu.make_async_copy(
            part, w_scr.at[pl.ds(pl.multiple_of(c * quarter, 64), quarter), :], sems.at[k]
        )
        for k, (part, c) in enumerate(((mine, core), (sib, 1 - core)))
    ]
    for c in copies:
        c.start()
    w_own = own[...].T
    at_own = pl.multiple_of(fi * half, 128)
    at_oth = pl.multiple_of((1 - fi) * half, 128)
    row_scr[:, pl.ds(at_own, half)] = small[6:8, :].astype(f32)
    row_scr[:, pl.ds(at_oth, half)] = small_oth[6:8, :].astype(f32)
    bias_scr[...] = jnp.zeros_like(bias_scr)
    for g in range(NG):

        @pl.when(g_id == g)
        def _(g=g):
            bias_scr[0:1, :GW] = row_scr[0:1, g * GW : (g + 1) * GW]
            bias_scr[0:1, 2 * GW :] = row_scr[1:2, g * GW : (g + 1) * GW]

    bias = bias_scr[...].T[:, :1]
    for c in copies:
        c.wait()
    w_oth = w_scr[...].T
    for j, x in enumerate((x0, x1, x2, x3)):
        cols = slice(j * block, (j + 1) * block)
        res = dot(w_own, x[:, pl.ds(at_own, half)], 1, 1)
        res += dot(w_oth, x[:, pl.ds(at_oth, half)], 1, 1)
        res = (res + bias).astype(bf16)
        q_ref[:, cols] = res[:GW]
        kv_ref[:, cols] = res[GW:]


def project(block, scal, xs, own, mine, sib, small, small_oth):
    rows = NG * block
    return pl.pallas_call(
        functools.partial(project_kernel, block),
        out_shape=(
            jax.ShapeDtypeStruct((GW, rows), bf16),
            jax.ShapeDtypeStruct((2 * GW, rows), bf16),
        ),
        in_specs=[SMEM] + vmem(7) + anyspec(2),
        out_specs=vmem(2),
        scratch_shapes=[
            pltpu.VMEM((2, 2 * own.shape[0]), f32),
            pltpu.VMEM((8, 3 * GW), f32),
            pltpu.VMEM(own.shape, bf16),
            pltpu.SemaphoreType.DMA((2,)),
        ],
        cost_estimate=CHEAP,
        compiler_params=params(),
        name="project",
    )(scal, *xs, own, small, small_oth, mine, sib)


def pack_kernel(*refs):
    out = refs[-1]
    n = out.shape[1]
    at = 0
    for ref in refs[:-1]:
        for k in range(ref.shape[0] // n):
            out[at : at + 1, :] = ref[k * n : (k + 1) * n].reshape(1, n)
            at += 1


def pack(vectors):
    n = vectors[0].shape[0]
    rows = sum(v.shape[0] for v in vectors) // n
    return pl.pallas_call(
        pack_kernel,
        out_shape=jax.ShapeDtypeStruct((rows, n), bf16),
        in_specs=vmem(len(vectors)),
        out_specs=vmem(1)[0],
        compiler_params=params(),
        name="pack",
    )(*vectors)


def tile_offset(t, scal, members, block):
    return pl.multiple_of(slot_of(t, scal[0], scal[1], members) * block, block)


UNROLL = 4


def key_loop(scal, j, block, tiles, init):
    low, high, inner_low, inner_high = (scal[2 + NG * i + j] for i in range(4))
    many = (inner_high - inner_low) // UNROLL
    rest = inner_low + UNROLL * many
    before = inner_low - low
    edges = before + high - rest

    def several(i, c):
        return tiles([inner_low + UNROLL * i + u for u in range(UNROLL)], None, c)

    def pair(i, c):
        ts, firsts = [], []
        for u in range(2):
            e = 2 * i + u
            t = jnp.minimum(jnp.where(e < before, low + e, rest + e - before), high - 1)
            ts.append(t)
            firsts.append(jnp.where(e < edges, t * block, -(1 << 30)))
        return tiles(ts, firsts, c)

    carry = lax.fori_loop(0, many, several, init)
    return lax.fori_loop(0, (edges + 1) // 2, pair, carry)


def inside(first, start, end, block):
    kpos = first + lax.broadcasted_iota(jnp.int32, (block, block), 0)
    return (kpos >= start) & (kpos < end)


def staged(n, first, second, third):
    one, two = {}, {}
    for i in range(n + 2):
        if i < n:
            one[i] = first(i)
        if 0 <= i - 1 < n:
            two[i - 1] = second(i - 1, one.pop(i - 1))
        if 0 <= i - 2 < n:
            third(i - 2, two.pop(i - 2))


def group_fwd_kernel(members, block, scal, st_ref, en_ref, q_ref, *rest):
    kv_refs = rest[:members]
    o_ref, lse_ref = rest[members : members + 2]
    ob_refs = rest[members + 2 : members + 2 + NG]
    k_scr, v_scr = rest[members + 2 + NG :]
    cols = NG * block
    for s in range(members):
        for h in range(HG):
            k_scr[h, s * cols : (s + 1) * cols, :] = kv_refs[s][h * HD : (h + 1) * HD, :].T
        v_scr[:, s * cols : (s + 1) * cols] = kv_refs[s][GW:, :]

    @pl.loop(0, NG)
    def _(j):
        cut = pl.ds(pl.multiple_of(j * block, block), block)
        start = st_ref[:, cut]
        end = en_ref[:, cut]
        qts = [q_ref[h * HD : (h + 1) * HD, cut] for h in range(HG)]

        def tiles(ts, firsts, carry):
            offs = [tile_offset(t, scal, members, block) for t in ts]
            allowed = firsts and [inside(first, start, end, block) for first in firsts]
            out = [None] * HG

            def first(h):
                return [dot(k_scr[h, pl.ds(off, block), :], qts[h]) for off in offs]

            def second(h, scores):
                top, total, acc = carry[h]
                if allowed:
                    scores = [jnp.where(a, s, NEG) for a, s in zip(allowed, scores)]
                new = top
                for s in scores:
                    new = jnp.maximum(new, jnp.max(s, axis=0, keepdims=True))
                alpha = jnp.exp2((top - new) * (SCALE * LOG2E))
                total = total * alpha
                probs = []
                for s in scores:
                    p = jnp.exp2((s - new) * (SCALE * LOG2E))
                    total += jnp.sum(p, axis=0, keepdims=True)
                    probs.append(p.astype(bf16))
                return probs, new, total, acc * alpha

            def third(h, state):
                probs, new, total, acc = state
                for p, off in zip(probs, offs):
                    acc += dot(v_scr[h * HD : (h + 1) * HD, pl.ds(off, block)], p)
                out[h] = (new, total, acc)

            staged(HG, first, second, third)
            return tuple(out)

        init = tuple(
            (
                jnp.full((1, block), NEG, f32),
                jnp.zeros((1, block), f32),
                jnp.zeros((HD, block), f32),
            )
            for _ in range(HG)
        )
        done = key_loop(scal, j, block, tiles, init)
        for h in range(HG):
            top, total, acc = done[h]
            o = acc / total
            o_ref[h * HD : (h + 1) * HD, cut] = o
            lse_ref[h : h + 1, cut] = top * (SCALE * LOG2E) + jnp.log2(total)

    for k in range(NG):
        ob_refs[k][...] = o_ref[:, k * block : (k + 1) * block].astype(bf16)


def group_fwd(members, block, scal, starts, ends, q, kvs):
    keys = members * NG * block
    rows = NG * block
    return pl.pallas_call(
        functools.partial(group_fwd_kernel, members, block),
        out_shape=(
            jax.ShapeDtypeStruct((GW, rows), f32),
            jax.ShapeDtypeStruct((HG, rows), f32),
        )
        + tuple(jax.ShapeDtypeStruct((GW, block), bf16) for _ in range(NG)),
        in_specs=[SMEM] + vmem(3 + members),
        out_specs=vmem(2 + NG),
        scratch_shapes=[
            pltpu.VMEM((HG, keys, HD), bf16),
            pltpu.VMEM((GW, keys), bf16),
        ],
        cost_estimate=CHEAP,
        compiler_params=params(),
        name="group_fwd",
    )(scal, starts, ends, q, *kvs)


def group_bwd_kernel(members, block, scal, st_ref, en_ref, q_ref, o_ref, lse_ref, *rest):
    do_refs = rest[:NG]
    kv_refs = rest[NG : NG + members]
    dq_ref = rest[NG + members]
    dkv_refs = rest[NG + members + 1 : NG + 2 * members + 1]
    k_scr, v_scr, dk_scr, dv_scr, do_scr = rest[NG + 2 * members + 1 :]
    cols = NG * block
    heads = [slice(h * HD, (h + 1) * HD) for h in range(HG)]
    for s in range(members):
        part = slice(s * cols, (s + 1) * cols)
        k_scr[:, part] = kv_refs[s][:GW, :]
        v_scr[:, part] = kv_refs[s][GW:, :]
    dk_scr[...] = jnp.zeros_like(dk_scr)
    dv_scr[...] = jnp.zeros_like(dv_scr)
    for k in range(NG):
        do_scr[:, k * block : (k + 1) * block] = do_refs[k][...]

    @pl.loop(0, NG)
    def _(j):
        cut = pl.ds(pl.multiple_of(j * block, block), block)
        start = st_ref[:, cut]
        end = en_ref[:, cut]
        per_head = []
        for h in range(HG):
            do = do_scr[heads[h], cut]
            delta = jnp.sum(do.astype(f32) * o_ref[heads[h], cut], axis=0, keepdims=True)
            per_head.append((q_ref[heads[h], cut], do, delta, lse_ref[h : h + 1, cut]))

        def tiles(ts, firsts, carry):
            out = list(carry)
            work = []
            for u, t in enumerate(ts):
                keys = pl.ds(tile_offset(t, scal, members, block), block)
                allowed = None if firsts is None else inside(firsts[u], start, end, block)
                work += [(h, keys, allowed) for h in range(HG)]

            def first(i):
                h, keys, _ = work[i]
                q, do, _, _ = per_head[h]
                return dot(k_scr[heads[h], keys], q, 0, 0), dot(v_scr[heads[h], keys], do, 0, 0)

            def second(i, pair):
                h, _, allowed = work[i]
                _, _, delta, lse = per_head[h]
                s, dp = pair
                p = jnp.exp2(s * (SCALE * LOG2E) - lse)
                if allowed is not None:
                    p = jnp.where(allowed, p, 0.0)
                return p.astype(bf16), (p * (dp - delta)).astype(bf16)

            def third(i, pair):
                h, keys, _ = work[i]
                q, do, _, _ = per_head[h]
                p, ds = pair
                dv_scr[heads[h], keys] += dot(do, p, 1, 1)
                dk_scr[heads[h], keys] += dot(q, ds, 1, 1)
                out[h] = out[h] + dot(k_scr[heads[h], keys], ds)

            staged(len(work), first, second, third)
            return tuple(out)

        init = tuple(jnp.zeros((HD, block), f32) for _ in range(HG))
        done = key_loop(scal, j, block, tiles, init)
        for h in range(HG):
            dq_ref[heads[h], cut] = (done[h] * SCALE).astype(bf16)

    for s in range(members):
        part = slice(s * cols, (s + 1) * cols)
        dkv_refs[s][:GW, :] = (dk_scr[:, part] * SCALE).astype(bf16)
        dkv_refs[s][GW:, :] = dv_scr[:, part].astype(bf16)


def group_bwd(members, block, scal, starts, ends, q, o, lse, dos, kvs):
    keys = members * NG * block
    rows = NG * block
    return pl.pallas_call(
        functools.partial(group_bwd_kernel, members, block),
        out_shape=(jax.ShapeDtypeStruct((GW, rows), bf16),)
        + tuple(jax.ShapeDtypeStruct((2 * GW, rows), bf16) for _ in range(members)),
        in_specs=[SMEM] + vmem(5 + NG + members),
        out_specs=vmem(1 + members),
        scratch_shapes=[
            pltpu.VMEM((GW, keys), bf16),
            pltpu.VMEM((GW, keys), bf16),
            pltpu.VMEM((GW, keys), f32),
            pltpu.VMEM((GW, keys), f32),
            pltpu.VMEM((GW, rows), bf16),
        ],
        cost_estimate=CHEAP,
        compiler_params=params(),
        name="group_bwd",
    )(scal, starts, ends, q, o, lse, *dos, *kvs)


def normalize(r, width):
    mean = jnp.sum(r, axis=1, keepdims=True) * (1.0 / width)
    centered = r - mean
    var = jnp.sum(centered * centered, axis=1, keepdims=True) * (1.0 / width)
    rstd = lax.rsqrt(var + eps)
    return centered * rstd, rstd


def norm_back(dy, hat, rstd, gain, width):
    dhat = dy * gain
    one = jnp.sum(dhat, axis=1, keepdims=True) * (1.0 / width)
    two = jnp.sum(dhat * hat, axis=1, keepdims=True) * (1.0 / width)
    return rstd * (dhat - one - hat * two)


INV_SQRT2 = 0.7071067811865476
INV_SQRT2PI = 0.3989422804014327


def middle_kernel(block, *refs):
    scal = refs[0]
    at = 1
    o_refs = refs[at : at + NG]
    at += NG
    x_ref, dy_ref, small, small_oth = refs[at : at + 4]
    at += 4
    out_parts = refs[at : at + 3]
    inner_parts = refs[at + 3 : at + 8]
    outer_parts = refs[at + 8 : at + 13]
    at += 13
    y_ref, dr_ref = refs[at : at + 2]
    at += 2
    do_refs = refs[at : at + NG]
    at += NG
    grad_outs = refs[at : at + 4]
    at += 4
    ot_scr, wout, winner, wouter, hbt, gt_scr, gp_scr, dot_scr, vec_ref, ib_ref, sums_ref, acc_ref = refs[at : at + 12]
    grad_refs = refs[at + 12 : at + 16]
    keeps, sends = grad_refs[:2], grad_refs[2:]
    sems = refs[at + 16]
    g_id, fi, core = scal[0], scal[1], scal[2]
    width = x_ref.shape[1]
    ffq = winner.shape[2]
    half = width // 2
    quarter = width // 4

    copies = []

    def load(src, dst):
        copies.append(pltpu.make_async_copy(src, dst, sems.at[len(copies)]))
        copies[-1].start()

    def rows_of(full):
        own = fi * (full // 2)
        oth = (1 - fi) * (full // 2)
        q = full // 4
        return (
            pl.ds(pl.multiple_of(own, 64), full // 2),
            pl.ds(pl.multiple_of(oth + core * q, 64), q),
            pl.ds(pl.multiple_of(oth + (1 - core) * q, 64), q),
        )

    for part, rows in zip(out_parts, rows_of(width)):
        load(part, wout.at[rows, :])
    own, mine, sib = (r.start for r in rows_of(width))
    unit = width // 16
    inner_rows = [pl.ds(own, 8 * unit)] + [
        pl.ds(pl.multiple_of(first + k * unit, 16), n * unit)
        for first in (mine, sib)
        for k, n in ((0, 1), (1, 3))
    ]
    for a in range(4):
        for part, rows in zip(inner_parts, inner_rows):
            load(part.at[:, a * ffq : (a + 1) * ffq], winner.at[a, rows, :])
    own, mine, sib = (r.start for r in rows_of(4 * ffq))
    unit = ffq // 4
    outer_rows = [pl.ds(own, 8 * unit)] + [
        pl.ds(pl.multiple_of(first + k * unit, 16), n * unit)
        for first in (mine, sib)
        for k, n in ((0, 1), (1, 3))
    ]
    for part, rows in zip(outer_parts, outer_rows):
        load(part, wouter.at[rows, :])

    for j in range(NG):
        row = pl.multiple_of(jnp.bitwise_xor(g_id, j) * GW, HD)
        ot_scr[pl.ds(row, GW), :] = o_refs[j][...]
    for side, y in ((small, fi), (small_oth, 1 - fi)):
        vec_ref[:, pl.ds(pl.multiple_of(y * half, 128), half)] = side[:8, :].astype(f32)
        for c in range(2):
            for k in range(2):
                ib_ref[pl.ds(2 * y + c, 1), k * half : (k + 1) * half] = side[
                    8 + 2 * c + k : 9 + 2 * c + k, :
                ].astype(f32)
    for c in copies[:3]:
        c.wait()
    vec = [vec_ref[i : i + 1, :] for i in range(8)]
    obias, gain1, shift1, outbias, gain2, shift2 = vec[:6]
    attn = ot_scr[...].T
    r1 = x_ref[...].astype(f32) + dot(attn, wout[...]) + obias
    hat1, rstd1 = normalize(r1, width)
    hn = hat1 * gain1 + shift1
    hb = hn.astype(bf16)
    hb_t = hb.T
    for y in range(2):
        for c in range(2):
            piece = hb_t[(2 * y + c) * quarter : (2 * y + c + 1) * quarter]

            @pl.when(core == c)
            def _(piece=piece, y=y):
                hbt[y * quarter : (y + 1) * quarter, :] = piece

            @pl.when(core != c)
            def _(piece=piece, y=y):
                hbt[half + y * quarter : half + (y + 1) * quarter, :] = piece

    for c in copies[3:]:
        c.wait()
    acc_ref[...] = hn + outbias

    @pl.loop(0, 4)
    def _(a):
        u = dot(hb, winner[a]) + ib_ref[pl.ds(a, 1), :]
        phi = 0.5 + 0.5 * lax.erf(u * INV_SQRT2)
        g = (u * phi).astype(bf16)
        gp_scr[a] = phi + u * (jnp.exp(u * u * -0.5) * INV_SQRT2PI)
        gt_scr[a] = g.T
        acc_ref[...] += dot(g, wouter[pl.ds(pl.multiple_of(a * ffq, ffq), ffq), :])

    z = acc_ref[...]
    hat2, rstd2 = normalize(z, width)
    y_ref[...] = (hat2 * gain2 + shift2).astype(bf16)
    dy = dy_ref[...].astype(f32)
    sums_ref[4:5, :] = jnp.sum(dy * hat2, axis=0, keepdims=True)
    sums_ref[5:6, :] = jnp.sum(dy, axis=0, keepdims=True)
    dz = norm_back(dy, hat2, rstd2, gain2, width)
    dzb = dz.astype(bf16)
    sums_ref[3:4, :] = jnp.sum(dzb.astype(f32), axis=0, keepdims=True)
    acc_ref[...] = dz

    @pl.loop(0, 4)
    def _(a):
        dg = dot(dzb, wouter[pl.ds(pl.multiple_of(a * ffq, ffq), ffq), :], 1, 1)
        du = (dg * gp_scr[a]).astype(bf16)
        sums_ref[pl.ds(6 + a, 1), :] = jnp.sum(du.astype(f32), axis=0, keepdims=True)
        acc_ref[...] += dot(du, winner[a], 1, 1)
        grad = dot(hbt[...], du).astype(bf16)
        rows = pl.ds(pl.multiple_of(a * quarter, 64), quarter)
        for y in range(2):
            keeps[0][y, rows] = grad[y * quarter : (y + 1) * quarter]
            sends[0][y, rows] = grad[half + y * quarter : half + (y + 1) * quarter]
        grad = dot(gt_scr[a], dzb).astype(bf16)
        mine = core == jnp.bitwise_and(a, 1)

        @pl.when(mine)
        def _():
            keeps[1][jnp.right_shift(a, 1), :ffq] = grad

        @pl.when(jnp.logical_not(mine))
        def _():
            sends[1][jnp.right_shift(a, 1), :ffq] = grad

    dh = acc_ref[...]
    stored = []

    def store(rows):
        for src, dst in zip(grad_refs, grad_outs):
            part = slice(*rows(src.shape[1]))
            sem = sems.at[len(copies) + len(stored)]
            stored.append(pltpu.make_async_copy(src.at[:, part], dst.at[:, part], sem))
            stored[-1].start()

    store(lambda n: (0, ffq))
    sums_ref[1:2, :] = jnp.sum(dh * hat1, axis=0, keepdims=True)
    sums_ref[2:3, :] = jnp.sum(dh, axis=0, keepdims=True)
    dr = norm_back(dh, hat1, rstd1, gain1, width)
    dr_ref[...] = dr
    dab = dr.astype(bf16)
    sums_ref[0:1, :] = jnp.sum(dab.astype(f32), axis=0, keepdims=True)
    for y in range(2):
        top = jnp.concatenate([sums_ref[0:6, :], sums_ref[6 + 2 * y : 8 + 2 * y, :]], axis=0)
        spare = jnp.concatenate([top, jnp.zeros((SPARE - 8, width), f32)], axis=0).astype(bf16)
        none = jnp.zeros((SPARE, width), bf16)

        @pl.when(core == 0)
        def _(y=y, spare=spare, none=none):
            keeps[0][y, 4 * quarter :] = spare
            sends[0][y, 4 * quarter :] = none

        @pl.when(core != 0)
        def _(y=y, spare=spare, none=none):
            keeps[0][y, 4 * quarter :] = none
            sends[0][y, 4 * quarter :] = spare

    dot_scr[...] = dot(wout[...], dab, 1, 1).astype(bf16)
    for j in range(NG):
        row = pl.multiple_of(jnp.bitwise_xor(g_id, j) * GW, HD)
        do_refs[j][...] = dot_scr[pl.ds(row, GW), :]
    grad = dot(ot_scr[...], dab).astype(bf16)
    for y in range(2):
        for c in range(2):
            piece = grad[(2 * y + c) * quarter : (2 * y + c + 1) * quarter]

            @pl.when(core == c)
            def _(piece=piece, y=y):
                keeps[1][y, ffq:] = piece

            @pl.when(core != c)
            def _(piece=piece, y=y):
                sends[1][y, ffq:] = piece

    store(lambda n: (ffq, n))
    for c in stored:
        c.wait()


def middle(block, scal, os, x, dy, small, small_oth, outs, inners, outers):
    width = x.shape[1]
    ffq = inners[0].shape[1] // 4
    q = width // 4
    grads = [
        jax.ShapeDtypeStruct((2, 4 * q + SPARE, ffq), bf16),
        jax.ShapeDtypeStruct((2, ffq + q, width), bf16),
    ]
    return pl.pallas_call(
        functools.partial(middle_kernel, block),
        out_shape=(
            jax.ShapeDtypeStruct((block, width), bf16),
            jax.ShapeDtypeStruct((block, width), f32),
        )
        + tuple(jax.ShapeDtypeStruct((GW, block), bf16) for _ in range(NG))
        + tuple(grads)
        + tuple(grads),
        in_specs=[SMEM] + vmem(NG + 4) + anyspec(13),
        out_specs=vmem(2 + NG) + anyspec(4),
        scratch_shapes=[
            pltpu.VMEM((width, block), bf16),
            pltpu.VMEM((width, width), bf16),
            pltpu.VMEM((4, width, ffq), bf16),
            pltpu.VMEM((4 * ffq, width), bf16),
            pltpu.VMEM((width, block), bf16),
            pltpu.VMEM((4, ffq, block), bf16),
            pltpu.VMEM((4, block, ffq), f32),
            pltpu.VMEM((width, block), bf16),
            pltpu.VMEM((8, width), f32),
            pltpu.VMEM((4, ffq), f32),
            pltpu.VMEM((16, width), f32),
            pltpu.VMEM((block, width), f32),
        ]
        + [pltpu.VMEM(g.shape, g.dtype) for g in grads + grads]
        + [
            pltpu.SemaphoreType.DMA((36,)),
        ],
        cost_estimate=CHEAP,
        compiler_params=params(60),
        name="middle",
    )(scal, *os, x, dy, small, small_oth, *outs, *inners, *outers)


def turn_kernel(scal, x0, x1, x2, x3, xt):
    core = scal[1]
    block, width = x0.shape
    half, quarter = width // 2, width // 4
    for j, x in enumerate((x0, x1, x2, x3)):
        cols = slice(j * block, (j + 1) * block)
        turned = x[...].T
        for y in range(2):
            for c in range(2):
                piece = turned[(2 * y + c) * quarter : (2 * y + c + 1) * quarter]

                @pl.when(core == c)
                def _(piece=piece, y=y):
                    xt[y * quarter : (y + 1) * quarter, cols] = piece

                @pl.when(core != c)
                def _(piece=piece, y=y):
                    xt[half + y * quarter : half + (y + 1) * quarter, cols] = piece


def turn(scal, xs):
    block, width = xs[0].shape
    return pl.pallas_call(
        turn_kernel,
        out_shape=jax.ShapeDtypeStruct((width, NG * block), bf16),
        in_specs=[SMEM] + vmem(NG),
        out_specs=vmem(1)[0],
        compiler_params=params(),
        name="turn",
    )(scal, *xs)


def qkv_grad_kernel(scal, xt, dq_ref, dkv_ref, keep, send, d_scr):
    g_id, core = scal[0], scal[2]
    d_scr[:GW, :] = dq_ref[...]
    d_scr[GW:, :] = dkv_ref[...]
    d = d_scr[...]
    quarter = xt.shape[0] // 4
    part = quarter // 2
    step = part + EXTRA
    grad = dot(xt[...], d, 1, 1).astype(bf16)
    ones = jnp.where(lax.broadcasted_iota(jnp.int32, (EXTRA, d.shape[1]), 0) == 0, 1.0, 0.0)
    sums = dot(ones.astype(bf16), d, 1, 1).astype(bf16)
    none = jnp.zeros_like(sums)
    for k, out in enumerate((keep, send)):
        for y in range(2):
            at = (2 * k + y) * quarter
            for x in range(2):
                out[y, x * step : x * step + part] = grad[at + x * part : at + (x + 1) * part]
                out[y, x * step + part : (x + 1) * step] = none
    for y in range(2):
        mine = jnp.right_shift(g_id, 1) == y

        @pl.when(mine & (core == 0))
        def _(y=y):
            keep[y, part:step] = sums

        @pl.when(mine & (core != 0))
        def _(y=y):
            send[y, part:step] = sums


def qkv_grad(scal, xt, dq, dkv):
    width, rows = xt.shape
    q = width // 4 + 2 * EXTRA
    return pl.pallas_call(
        qkv_grad_kernel,
        out_shape=(
            jax.ShapeDtypeStruct((2, q, 3 * GW), bf16),
            jax.ShapeDtypeStruct((2, q, 3 * GW), bf16),
        ),
        in_specs=[SMEM] + vmem(3),
        out_specs=vmem(2),
        scratch_shapes=[pltpu.VMEM((3 * GW, rows), bf16)],
        compiler_params=params(),
        name="qkv_grad",
    )(scal, xt, dq, dkv)


def each_part(scal, fn):
    xi, core = scal[1], scal[2]
    for c in range(2):
        for x in range(2):
            fn(c, x, jnp.bitwise_xor(core, c) * 2 + jnp.bitwise_xor(xi, x))


def unpack_kernel(place, scal, *refs):
    parts, outs, bias_ref = refs[0], refs[1:4], refs[4]
    rows = parts.shape[2] - EXTRA
    fi = place[1]

    def put(c, x, s):
        at = (2 * c + x) * rows
        for g in range(NG):
            v = parts[s, g, :rows].astype(f32)
            for part in range(3):
                outs[part][at : at + rows, g * GW : (g + 1) * GW] = v[
                    :, part * GW : (part + 1) * GW
                ]
        if (c, x) == (0, 0):
            for k in range(2):
                row = parts[s, 2 * fi + k, rows:].astype(f32)
                bias_ref[0:1, k * GW : (k + 1) * GW] = row[:1, :GW]
                bias_ref[1:2, k * GW : (k + 1) * GW] = row[:1, 2 * GW :]

    each_part(scal, put)


def spread_rows(segments, first, v):
    base = 0
    for n, place in segments:
        lo, hi = max(first, base), min(first + v.shape[0], base + n)
        if lo < hi:
            place(lo - base, v[lo - first : hi - first])
        base += n


def finish_kernel(scal, *refs):
    parts_a, whole_b = refs[:2]
    outer_ref, inner_ref, out_ref, vec_ref = refs[2:]
    ffq = inner_ref.shape[1] // 4
    quarter = inner_ref.shape[0] // 2
    g_id = scal[0]
    n_a, n_b = parts_a.shape[2], whole_b.shape[1]

    def put_a(c, x, s):
        def outer(row, v):
            outer_ref[c * ffq + row : c * ffq + row + v.shape[0], :] = v

        def out(row, v):
            out_ref[c * quarter + row : c * quarter + row + v.shape[0], :] = v

        for g in range(NG):
            j = jnp.bitwise_xor(g_id, g)
            v = parts_a[s, jnp.bitwise_and(j, 1) * 2 + jnp.right_shift(j, 1)].astype(f32)
            spread_rows(((ffq, outer), (quarter, out)), (NG * x + g) * n_a, v)

    each_part(scal, put_a)
    for i in range(whole_b.shape[0]):
        g, x, c = i >> 2, i >> 1 & 1, i & 1
        def inner(a, row, v, c=c):
            at = c * quarter + row
            inner_ref[at : at + v.shape[0], a * ffq : (a + 1) * ffq] = v

        def sums(row, v, c=c):
            if c == 0 and row < 8:
                vec_ref[row : min(8, row + v.shape[0]), :] = v[: 8 - row]

        spread_rows(
            tuple((quarter, functools.partial(inner, a)) for a in range(4)) + ((SPARE, sums),),
            (NG * x + g) * n_b,
            whole_b[i].astype(f32),
        )


def ending_kernel(place, spot, *refs):
    parts, whole_b, parts_q = refs[:4], refs[4], refs[5:9]
    dr_ref, d_refs, w_parts = refs[9], refs[10 : 10 + 2 * NG], refs[10 + 2 * NG : 13 + 2 * NG]
    outs = refs[13 + 2 * NG : 21 + 2 * NG]
    dx_ref = refs[21 + 2 * NG]
    staged_refs = refs[22 + 2 * NG : 30 + 2 * NG]
    w_scr, d_scr, a_scr, q_scr, sems = refs[30 + 2 * NG :]
    g_id, fi, core = place[0], place[1], place[2]
    width = w_scr.shape[0]
    q = width // 4
    oth = (1 - fi) * 2 * q
    rows = (
        pl.ds(pl.multiple_of(fi * 2 * q, 64), 2 * q),
        pl.ds(pl.multiple_of(oth + core * q, 64), q),
        pl.ds(pl.multiple_of(oth + (1 - core) * q, 64), q),
    )
    loads = [
        pltpu.make_async_copy(p, w_scr.at[r, :], sems.at[i])
        for i, (p, r) in enumerate(zip(w_parts, rows))
    ]
    pieces = [
        pltpu.make_async_copy(src, scr.at[s], sems.at[11 + 4 * k + s])
        for k, (group, scr) in enumerate(((parts, a_scr), (parts_q, q_scr)))
        for s, src in enumerate(group)
    ]
    for c in pieces + loads:
        c.start()
    stores = [
        pltpu.make_async_copy(src, dst, sems.at[3 + i])
        for i, (src, dst) in enumerate(zip(staged_refs, outs))
    ]
    for c in pieces[:4]:
        c.wait()
    finish_kernel(spot, a_scr, whole_b, *staged_refs[:4])
    for c in stores[:4]:
        c.start()
    for c in pieces[4:]:
        c.wait()
    unpack_kernel(place, spot, q_scr, *staged_refs[4:])
    for c in stores[4:]:
        c.start()
    for j in range(NG):
        base = jnp.bitwise_xor(g_id, j) * GW
        for part in range(3):
            at = pl.multiple_of(part * width + base, HD)
            src = d_refs[j][...] if part == 0 else d_refs[NG + j][(part - 1) * GW : part * GW, :]
            d_scr[pl.ds(at, GW), :] = src
    for c in loads:
        c.wait()
    dx_ref[...] = dr_ref[...] + dot(w_scr[...], d_scr[...]).T
    for c in stores:
        c.wait()


def ending(place, spot, parts_a, whole_b, parts_q, dr, d_parts, w_parts, shapes):
    block, width = dr.shape
    wide = [
        *shapes,
        (8, width),
        *((width // 2, width) for _ in range(3)),
        (2, 2 * GW),
    ]
    return pl.pallas_call(
        ending_kernel,
        out_shape=tuple(jax.ShapeDtypeStruct(s, f32) for s in wide)
        + (jax.ShapeDtypeStruct((block, width), f32),),
        in_specs=[SMEM, SMEM] + anyspec(4) + vmem(1) + anyspec(4) + vmem(1 + 2 * NG) + anyspec(3),
        out_specs=anyspec(8) + vmem(1),
        scratch_shapes=[pltpu.VMEM(s, f32) for s in wide]
        + [
            pltpu.VMEM((width, 3 * width), bf16),
            pltpu.VMEM((3 * width, block), bf16),
            pltpu.VMEM((4,) + parts_a[0].shape, bf16),
            pltpu.VMEM((4,) + parts_q[0].shape, bf16),
            pltpu.SemaphoreType.DMA((19,)),
        ],
        cost_estimate=CHEAP,
        compiler_params=params(60),
        name="ending",
    )(place, spot, *parts_a, whole_b, *parts_q, dr, *d_parts, *w_parts)


def fast_device(
    tokens,
    query_weight,
    query_bias,
    key_weight,
    value_weight,
    value_bias,
    out_weight,
    out_bias,
    first_gain,
    first_shift,
    inner_weight,
    inner_bias,
    outer_weight,
    outer_bias,
    second_gain,
    second_shift,
    doc_lengths,
    grad_output,
):
    block = tokens.shape[1]
    width = tokens.shape[2]
    ctx = lax.axis_size("ctx")
    members = ctx // NG
    ci = lax.axis_index("ctx")
    fi = lax.axis_index("fsdp")
    g_id = ci // members
    m_id = ci % members
    core = ci % 2
    xi = m_id // 2
    half = width // 2
    tie = lax.optimization_barrier

    def zswap(v, j):
        return swap(v, "ctx", j * members)

    def xswap(v):
        return swap(v, "ctx", 2)

    def cswap(v):
        return swap(v, "ctx", 1)

    def yswap(v):
        return swap(v, "fsdp", 1)

    local = tokens[0]
    x2 = zswap(local, 2)
    x1 = zswap(local, 1)
    w_own = jnp.concatenate(
        [
            lax.dynamic_slice_in_dim(w, g_id * GW, GW, 1)
            for w in (query_weight, key_weight, value_weight)
        ],
        axis=1,
    )
    small = pack(
        [
            out_bias,
            first_gain,
            first_shift,
            outer_bias,
            second_gain,
            second_shift,
            query_bias,
            value_bias,
            inner_bias,
        ]
    )

    def half_of(w):
        rows = w.shape[0] // 2
        return lax.dynamic_slice_in_dim(w, core * rows, rows, 0)

    w_mine = yswap(half_of(w_own))
    out_mine = yswap(half_of(out_weight))
    w_sib = cswap(w_mine)
    out_mine, small, w_mine, w_sib, x2, x1, inner_raw, outer_raw, doc_lengths = tie(
        (out_mine, small, w_mine, w_sib, x2, x1, inner_weight, outer_weight, doc_lengths)
    )
    x3 = zswap(x2, 1)
    small_oth = yswap(small)
    inner_half, outer_half = half_of(inner_raw), half_of(outer_raw)
    cut = inner_half.shape[0] // 4
    inner_one = yswap(inner_half[:cut])

    doc_ends = jnp.cumsum(doc_lengths[0])
    first = jnp.stack([(jnp.bitwise_xor(g_id, j) * members + m_id) * block for j in range(NG)])
    places = (first[:, None] + jnp.arange(block, dtype=jnp.int32)[None, :]).reshape(-1)
    before = places[:, None] >= doc_ends[None, :]
    starts = jnp.max(jnp.where(before, doc_ends[None, :], 0), axis=1).astype(jnp.int32)
    ends = jnp.min(jnp.where(before, ctx * block, doc_ends[None, :]), axis=1).astype(jnp.int32)
    low = starts.reshape(NG, block)[:, 0] // block
    high = (ends.reshape(NG, block)[:, -1] + block - 1) // block
    plain_low = (starts.reshape(NG, block)[:, -1] + block - 1) // block
    plain_high = ends.reshape(NG, block)[:, 0] // block
    whole = plain_low < plain_high
    plain_low = jnp.where(whole, plain_low, high)
    plain_high = jnp.where(whole, plain_high, high)
    scal = jnp.concatenate(
        [jnp.stack([m_id, g_id]), low, high, plain_low, plain_high]
    ).astype(jnp.int32)
    starts = starts[None]
    ends = ends[None]
    place = jnp.stack([g_id, fi, core]).astype(jnp.int32)
    spot = jnp.stack([g_id, xi, core]).astype(jnp.int32)
    dev = jnp.stack([fi, core]).astype(jnp.int32)
    tied = (small_oth, place, spot, dev, x3, inner_one, inner_half, outer_half, scal, starts, ends)
    small_oth, place, spot, dev, x3, inner_one, inner_half, outer_half, scal, starts, ends = tie(tied)

    xs = [local, x1, x2, x3]
    q_t, kv = project(block, place, xs, w_own, w_mine, w_sib, small, small_oth)

    kv_x = xswap(kv)
    inner_two = yswap(inner_half[cut:])
    cut = outer_half.shape[0] // 4
    outer_one = yswap(outer_half[:cut])
    sibs = [cswap(out_mine), cswap(inner_one)]
    tied = tie((kv_x, inner_two, outer_one) + tuple(sibs))
    (kv_x, inner_two, outer_one), sibs = tied[:3], list(tied[3:])
    kv_c = cswap(kv)
    kv_xc = cswap(kv_x)
    kv, kv_c, kv_x, kv_xc, inner_two, outer_one, outer_half = tie(
        (kv, kv_c, kv_x, kv_xc, inner_two, outer_one, outer_half)
    )
    kvs = [kv, kv_c, kv_x, kv_xc]
    outer_two = yswap(outer_half[cut:])
    sibs += [cswap(inner_two), cswap(outer_one)]
    res = group_fwd(members, block, scal, starts, ends, q_t, kvs)
    qkv_shard = jnp.concatenate([query_weight, key_weight, value_weight], axis=1)
    qkv_half = half_of(qkv_shard)
    tied = tie(tuple(res) + (outer_two, qkv_shard, qkv_half) + tuple(sibs))
    res, (outer_two, qkv_shard, qkv_half), sibs = tied[: 2 + NG], tied[2 + NG : 5 + NG], list(tied[5 + NG :])
    o_t, lse = res[:2]
    o_cols = list(res[2:])
    o_parts = [o_cols[0]] + [zswap(o_cols[j], j) for j in range(1, NG)]
    sibs.append(cswap(outer_two))
    tied = tie(tuple(o_parts) + (sibs[-1], qkv_half))
    o_parts, sibs[-1], qkv_half = list(tied[:NG]), tied[NG], tied[NG + 1]
    outs = (out_weight, out_mine, sibs[0])
    inners = (inner_weight, inner_one, inner_two, sibs[1], sibs[2])
    outers = (outer_weight, outer_one, outer_two, sibs[3], sibs[4])
    qkv_mine = yswap(qkv_half)

    mid = middle(block, place, o_parts, local, grad_output[0], small, small_oth, outs, inners, outers)
    tied = tie(tuple(mid) + (qkv_mine,))
    mid, qkv_mine = tied[:-1], tied[-1]
    output, d_first = mid[:2]
    dos = list(mid[2 : 2 + NG])
    keep_a, keep_b, send_a, send_b = mid[2 + NG :]

    state = [output]

    def then(v):
        v, _ = tie((v, state[0]))
        state[0] = v
        return v

    def rows_at(v, index, parts, axis=0):
        n = v.shape[axis] // parts
        return lax.dynamic_slice_in_dim(v, index * n, n, axis)

    def low_sum(terms, cut):
        return then(sum(cut(t).astype(f32) for t in terms).astype(bf16))

    z1 = g_id % 2
    z2 = g_id // 2

    keep_a, keep_b, send_a, send_b = keep_b, keep_a, send_b, send_a
    core_a = cswap(send_a)
    core_b = cswap(send_b)
    dos = [dos[0]] + [zswap(dos[j], j) for j in range(1, NG)]
    terms_b = [keep_b, core_b]
    terms_a = [keep_a, core_a]
    send_a = low_sum(terms_a, lambda v: pick(v, 1 - fi))
    send_b = low_sum(terms_b, lambda v: rows_at(v, 1 - xi, 2, 1))
    tied = tie(tuple(dos) + (send_a, send_b))
    dos, (send_a, send_b) = list(tied[:NG]), tied[NG:]
    got_a = yswap(send_a)
    got_b = xswap(send_b)
    res = group_bwd(members, block, scal, starts, ends, q_t, o_t, lse, dos, kvs)
    tied = tie(tuple(res) + (got_a, got_b))
    res, (got_a, got_b) = tied[:-2], tied[-2:]
    state[0] = got_b
    terms_a = [pick(t, fi) for t in terms_a] + [got_a]
    terms_b = [rows_at(t, xi, 2, 1) for t in terms_b] + [got_b]

    send_a = low_sum(terms_a, lambda v: rows_at(v, 1 - xi, 2))
    send_b = low_sum(terms_b, lambda v: pick(v, 1 - fi))
    got_a, got_b = xswap(send_a), yswap(send_b)
    dq, slots = res[0], res[1:]
    k1, k3 = cswap(slots[1]), cswap(slots[3])
    qkv_sib = cswap(qkv_mine)
    got_a, got_b, k1, k3, qkv_sib = tie((got_a, got_b, k1, k3, qkv_sib))
    terms_a = [rows_at(t, xi, 2) for t in terms_a] + [got_a]
    terms_b = [pick(t, fi) for t in terms_b] + [got_b]
    sum_a = sum(t.astype(f32) for t in terms_a).astype(bf16).reshape(NG, -1, width)
    sum_b = sum(t.astype(f32) for t in terms_b).astype(bf16).reshape(NG, -1, width)
    n_a, n_b = sum_a.shape[1], sum_b.shape[1]
    chunk = then(jnp.concatenate([sum_a, sum_b], axis=1).reshape(-1, width))
    columns = [[m + members * g for g in range(NG)] for m in range(members)]
    piece = lax.psum_scatter(
        chunk, "ctx", scatter_dimension=0, tiled=True, axis_index_groups=columns
    )
    got_kv = xswap(low_sum([slots[2], k3], lambda v: v))
    xt = turn(dev, tie(tuple(xs) + (state[0],))[:NG])
    dq_parts = [dq[:, j * block : (j + 1) * block] for j in range(NG)]
    dq_parts = tie(tuple(dq_parts) + (state[0],))[:NG]
    dq_parts = [dq_parts[0]] + [zswap(dq_parts[j], j) for j in range(1, NG)]
    tied = tie((got_kv, xt) + tuple(dq_parts))
    got_kv, xt, dq_parts = tied[0], tied[1], list(tied[2:])
    dkv = low_sum([slots[0], k1, got_kv], lambda v: v)
    dkv_parts = [dkv[:, j * block : (j + 1) * block] for j in range(NG)]
    keep_q, send_q = qkv_grad(place, xt, dq, dkv)
    terms_q = [keep_q, cswap(send_q)]
    got_q = yswap(low_sum(terms_q, lambda v: pick(v, 1 - fi)))
    terms_q = [pick(t, fi) for t in terms_q] + [got_q]

    piece = tie((piece, state[0]))[0]
    piece_a = piece[:n_a]
    whole_b = lax.all_gather(piece[n_a:], "ctx", axis=0)
    far_a = zswap(piece_a, 2)
    got_q = xswap(low_sum(terms_q, lambda v: rows_at(v, 1 - xi, 2)))
    far_a = tie((far_a, state[0]))[0]
    pair_a = then(jnp.stack([piece_a, far_a]))
    near_a = zswap(pair_a, 1)
    got_q = tie((got_q, state[0]))[0]
    terms_q = [rows_at(t, xi, 2) for t in terms_q] + [got_q]
    piece_q = low_sum(terms_q, lambda v: v)
    far_q = zswap(piece_q, 2)
    near_a = tie((near_a, state[0]))[0]
    col_a = then(jnp.stack([pair_a, near_a]))
    side_a = xswap(col_a)
    far_q = tie((far_q, state[0]))[0]
    piece_q = then(ordered(z2, piece_q, far_q))
    near_q = zswap(piece_q, 1)
    piece_q = then(ordered(z1, piece_q, near_q).transpose(1, 0, 2, 3).reshape(NG, -1, 3 * GW))
    side_q = xswap(piece_q)
    dkv_parts = tie(tuple(dkv_parts) + (state[0],))[:NG]
    dkv_parts = [dkv_parts[0]] + [zswap(dkv_parts[j], j) for j in range(1, NG)]
    tied = tie((side_a, side_q) + tuple(dkv_parts))
    side_a, side_q, dkv_parts = tied[0], tied[1], tied[2:]
    parts_q = [piece_q, side_q, cswap(piece_q), cswap(side_q)]
    core_a, core_side = cswap(col_a), cswap(side_a)
    tied = tie(tuple(parts_q) + (core_a, core_side))
    parts_q, core_a, core_side = tied[:4], tied[4], tied[5]
    parts_a = [v.reshape(NG, n_a, width) for v in (col_a, side_a, core_a, core_side)]
    tied = tie(tuple(parts_q) + tuple(parts_a) + (whole_b,) + tuple(dq_parts) + tuple(dkv_parts))
    parts_q, parts_a, whole_b, d_parts = tied[:4], tied[4:8], tied[8], tied[9:]
    (
        grad_outer,
        grad_inner,
        grad_out,
        vecs,
        grad_query,
        grad_key,
        grad_value,
        bias_rows,
        grad_input,
    ) = ending(
        place,
        spot,
        parts_a,
        whole_b,
        parts_q,
        d_first,
        d_parts,
        (qkv_shard, qkv_mine, qkv_sib),
        (outer_weight.shape, inner_weight.shape, out_weight.shape),
    )

    mine = lax.dynamic_slice_in_dim(vecs, fi * half, half, 1)
    return (
        output[None],
        grad_input[None],
        grad_query,
        bias_rows[0],
        grad_key,
        grad_value,
        bias_rows[1],
        grad_out,
        mine[0],
        mine[1],
        mine[2],
        grad_inner,
        vecs[6:8].reshape(-1),
        grad_outer,
        mine[3],
        mine[4],
        mine[5],
    )


def solution(mesh):
    placed = (
        P("fsdp", "ctx", None),
        P("fsdp", None),
        P("fsdp"),
        P("fsdp", None),
        P("fsdp", None),
        P("fsdp"),
        P("fsdp", None),
        P("fsdp"),
        P("fsdp"),
        P("fsdp"),
        P("fsdp", None),
        P("fsdp"),
        P("fsdp", None),
        P("fsdp"),
        P("fsdp"),
        P("fsdp"),
        P("fsdp", None),
        P("fsdp", "ctx", None),
    )
    quick = mesh.shape["fsdp"] == 2 and mesh.shape["ctx"] == 4 * NG
    return jax.shard_map(
        fast_device if quick else on_device,
        mesh=mesh,
        in_specs=placed,
        out_specs=(
            P("fsdp", "ctx", None),
            P("fsdp", "ctx", None),
            P("fsdp", None),
            P("fsdp"),
            P("fsdp", None),
            P("fsdp", None),
            P("fsdp"),
            P("fsdp", None),
            P("fsdp"),
            P("fsdp"),
            P("fsdp"),
            P("fsdp", None),
            P("fsdp"),
            P("fsdp", None),
            P("fsdp"),
            P("fsdp"),
            P("fsdp"),
        ),
        check_vma=False,
    )
```

profile of v0, /device:TPU:1, one launch (start us, length us, event | category | flops | bytes accessed | tf_op | source)
XLA Modules:
  0.0 342.5 jit_solution(8213382170888777958)
XLA Ops:
  7.2 3.2 collective-permute-start.3
  10.4 1.3 collective-permute-start.4
  14.1 1.8 constant_dynamic-slice_fusion.8
  21.7 1.4 pack.1.small.refs_7_
  23.2 1.8 collective-permute-done.1.mine
  25.0 3.9 %collective-permute-start.2 = (bf16[192,576]{1,0:T(8,128)(2,1)}, bf16[192,576]{1,0:T(8,128)(2,1)}, u32[]{:S(2)}, u32[]{:S(2)}) collective-permute-start(bf16[192,576]{1,0:T(8,128)(2,1)} %collective-permute-done.1.mine), channel_id=1, source_target_pairs={{0,2},{2,0},{4,6},{6,4},{8,10},{10,8},{12,14},{14,12},{16,18},{18,... | collective-permute-start | bytes 663560 | tf_op jit(solution)/shard_map/ppermute | solution.py:44
  34.8 1.3 collective-permute-start.7
  36.7 1.4 constant_dynamic-slice_fusion.3
  38.7 3.0 collective-permute-done.5.small_oth.refs_8_
  41.7 2.8 collective-permute-done.6.x3
  45.2 5.0 %project.1 = (bf16[192,1024]{1,0:T(8,128)(2,1)}, bf16[384,1024]{1,0:T(8,128)(2,1)}) custom-call(s32[3]{0:T(128)} %get-tuple-element.202.scal.refs_0_.place, bf16[256,768]{1,0:T(8,128)(2,1)} %bitcast.72, bf16[256,768]{1,0:T(8,128)(2,1)} %copy-done.12, bf16[256,768]{1,0:T(8,128)(2,1)} %copy-done.11, bf16[256,768]{1,0:T(8,128)(2,1)} %copy-done.13, ...), custom_call_target="tpu_custom_call" | custom-call | flops 1 | bytes 1 | tf_op jit(solution)/shard_map/project/pallas_call | solution.py:542
  51.5 3.6 %collective-permute-start.12 = (bf16[192,768]{1,0:T(8,128)(2,1)}, bf16[192,768]{1,0:T(8,128)(2,1)S(1)}, u32[]{:S(2)}, u32[]{:S(2)}) collective-permute-start(bf16[192,768]{1,0:T(8,128)(2,1)} %collective-permute-done.refs_10_), channel_id=1, source_target_pairs={{0,2},{2,0},{4,6},{6,4},{8,10},{10,8},{12,14},{14,12},{16,18},{18,... | collective-permute-start | bytes 884744 | tf_op jit(solution)/shard_map/ppermute | solution.py:44
  56.9 11.8 %collective-permute-done.11.refs_18_ = bf16[192,768]{1,0:T(8,128)(2,1)S(1)} collective-permute-done((bf16[192,768]{1,0:T(8,128)(2,1)S(1)}, bf16[192,768]{1,0:T(8,128)(2,1)S(1)}, u32[]{:S(2)}, u32[]{:S(2)}) %collective-permute-start.11) | collective-permute-done | bytes 294944 | tf_op jit(solution)/shard_map/ppermute | solution.py:44
  68.8 4.3 %collective-permute-start.14 = (bf16[384,1024]{1,0:T(8,128)(2,1)S(1)}, bf16[384,1024]{1,0:T(8,128)(2,1)S(1)}, u32[]{:S(2)}, u32[]{:S(2)}) collective-permute-start(bf16[384,1024]{1,0:T(8,128)(2,1)S(1)} %collective-permute-done.9.rest_2_.rest_6_), channel_id=1, source_target_pairs={{0,2},{2,0},{4,6},{6,4},{8,10},{10,8},{12,14},{14,12},{16,18},{18,... | collective-permute-start | bytes 2359304 | tf_op jit(solution)/shard_map/ppermute | solution.py:44
  73.1 1.9 collective-permute-done.14.rest_3_.rest_7_
  77.0 18.1 %group_fwd.1 = (f32[192,1024]{1,0:T(8,128)}, f32[3,1024]{1,0:T(4,128)}, bf16[192,256]{1,0:T(8,128)(2,1)}, bf16[192,256]{1,0:T(8,128)(2,1)}, bf16[192,256]{1,0:T(8,128)(2,1)}, /*index=5*/bf16[192,256]{1,0:T(8,128)(2,1)}) custom-call(s32[18]{0:T(128)} %concatenate.13.scal, s32[1,1024]{1,0:T(1,128)} %bitcast.95, s32[1,1024]{1,0:T(1,128)} %bitcast.93, ...), custom_call_target="tpu_custom_call" | custom-call | flops 1 | bytes 1 | tf_op jit(solution)/shard_map/group_fwd/pallas_call | solution.py:704
  97.5 1.5 collective-permute-start.19
  99.0 1.9 collective-permute-start.20
  100.9 2.1 collective-permute-done.18.refs_2_
  103.0 3.9 %collective-permute-done.19.refs_3_ = bf16[192,256]{1,0:T(8,128)(2,1)S(1)} collective-permute-done((bf16[192,256]{1,0:T(8,128)(2,1)}, bf16[192,256]{1,0:T(8,128)(2,1)S(1)}, u32[]{:S(2)}, u32[]{:S(2)}) %collective-permute-start.19) | collective-permute-done | bytes 98336 | tf_op jit(solution)/shard_map/ppermute | solution.py:44
  107.9 22.5 %middle.1 = (bf16[256,768]{1,0:T(8,128)(2,1)}, f32[256,768]{1,0:T(8,128)}, bf16[192,256]{1,0:T(8,128)(2,1)}, bf16[192,256]{1,0:T(8,128)(2,1)}, bf16[192,256]{1,0...) custom-call(s32[3]{0:T(128)} %get-tuple-element.202.scal.refs_0_.pla, ...), custom_call_target="tpu_custom_call" | custom-call | flops 1 | bytes 1 | tf_op jit(solution)/shard_map/middle/pallas_call | solution.py:1041
  130.4 2.0 collective-permute-start.26
  132.5 1.6 collective-permute-start.23
  134.2 2.1 collective-permute-start.25
  136.3 5.2 %collective-permute-done.27 = bf16[2,832,768]{2,1,0:T(8,128)(2,1)} collective-permute-done((bf16[2,832,768]{2,1,0:T(8,128)(2,1)}, bf16[2,832,768]{2,1,0:T(8,128)(2,1)}, u32[]{:S(2)}, u32[]{:S(2)}) %collective-permute-start.27) | collective-permute-done | bytes 2555936 | tf_op jit(solution)/shard_map/ppermute | solution.py:44
  141.5 3.0 add_convert_fusion.1
  144.5 2.8 fusion
  150.6 22.8 %group_bwd.1 = (bf16[192,1024]{1,0:T(8,128)(2,1)}, bf16[384,1024]{1,0:T(8,128)(2,1)}, bf16[384,1024]{1,0:T(8,128)(2,1)}, bf16[384,1024]{1,0:T(8,128)(2,1)}, bf16[384,1024]{1,0:T(8,128)(2,1)}) custom-call(s32[18]{0:T(128)} %concatenate.13.scal, s32[1,1024]{1,0:T(1,128)} %bitcast.96, s32[1,1024]{1,0:T(1,128)} %bitcast.94, ...), custom_call_target="tpu_custom_call" | custom-call | flops 1 | bytes 1 | tf_op jit(solution)/shard_map/group_bwd/pallas_call | solution.py:798
  173.3 4.4 %collective-permute-done.29 = bf16[2,416,768]{2,1,0:T(8,128)(2,1)} collective-permute-done((bf16[2,416,768]{2,1,0:T(8,128)(2,1)}, bf16[2,416,768]{2,1,0:T(8,128)(2,1)}, u32[]{:S(2)}, u32[]{:S(2)}) %collective-permute-start.29) | collective-permute-done | bytes 1277984 | tf_op jit(solution)/shard_map/ppermute | solution.py:44
  177.7 3.6 %collective-permute-done.28 = bf16[960,768]{1,0:T(8,128)(2,1)} collective-permute-done((bf16[960,768]{1,0:T(8,128)(2,1)}, bf16[960,768]{1,0:T(8,128)(2,1)}, u32[]{:S(2)}, u32[]{:S(2)}) %collective-permute-start.28) | collective-permute-done | bytes 1474592 | tf_op jit(solution)/shard_map/ppermute | solution.py:44
  182.5 2.7 fusion.3
  186.3 2.7 fusion.5
  190.0 14.5 %collective-permute-done.31 = bf16[416,768]{1,0:T(8,128)(2,1)} collective-permute-done((bf16[416,768]{1,0:T(8,128)(2,1)}, bf16[416,768]{1,0:T(8,128)(2,1)}, u32[]{:S(2)}, u32[]{:S(2)}) %collective-permute-start.31) | collective-permute-done | bytes 639008 | tf_op jit(solution)/shard_map/ppermute | solution.py:44
  204.5 2.2 fusion.4
  206.7 2.1 fusion.2
  210.2 1.4 add_convert_fusion.3
  212.6 1.6 collective-permute-start.36
  214.2 2.1 collective-permute-start.38
  216.3 3.3 turn.1.xt
  219.7 8.8 %collective-permute-done.37.refs_12_ = bf16[192,256]{1,0:T(8,128)(2,1)S(1)} collective-permute-done((bf16[192,256]{1,0:T(8,128)(2,1)S(1)}, bf16[192,256]{1,0:T(8,128)(2,1)S(1)}, u32[]{:S(2)}, u32[]{:S(2)}) %collective-permute-start.37) | collective-permute-done | bytes 98336 | tf_op jit(solution)/shard_map/ppermute | solution.py:44
  229.2 2.4 add_convert_fusion.2.dkv_ref
  231.6 4.6 %qkv_grad.1 = (bf16[2,208,576]{2,1,0:T(8,128)(2,1)}, bf16[2,208,576]{2,1,0:T(8,128)(2,1)}) custom-call(s32[3]{0:T(128)} %get-tuple-element.202.scal.refs_0_.place, bf16[768,1024]{1,0:T(8,128)(2,1)} %turn.1.xt, bf16[192,1024]{1,0:T(8,128)(2,1)} %get-tuple-element.304.dq_ref, bf16[384,1024]{1,0:T(8,128)(2,1)} %add_convert_fusion.2.dkv_ref), custom_call_target="tpu_custom_call" | custom-call | tf_op jit(solution)/shard_map/qkv_grad/pallas_call | solution.py:1141
  236.3 2.5 collective-permute-start.39
  238.8 1.8 collective-permute-done.39
  241.6 5.9 %reduce-scatter.2.cloned.1.call-done = bf16[224,768]{1,0:T(8,128)(2,1)} async-done(((bf16[896,768]{1,0:T(8,128)(2,1)}), bf16[224,768]{1,0:T(8,128)(2,1)}) %reduce-scatter.2.cloned.1.call-update) | async-done | bytes 344080 | tf_op jit(solution)/shard_map/reduce_scatter | solution.py:1513
  247.5 1.6 slice.98
  251.0 1.9 collective-permute-start.42
  253.0 2.8 collective-permute-done.40
  255.9 4.5 %collective-permute-done.42 = bf16[120,768]{1,0:T(8,128)(2,1)S(1)} collective-permute-done((bf16[120,768]{1,0:T(8,128)(2,1)S(1)}, bf16[120,768]{1,0:T(8,128)(2,1)S(1)}, u32[]{:S(2)}, u32[]{:S(2)}) %collective-permute-start.42) | collective-permute-done | bytes 184352 | tf_op jit(solution)/shard_map/ppermute | solution.py:44
  262.3 2.8 collective-permute-done.41
  265.2 4.6 %collective-permute-start.43 = (bf16[104,576]{1,0:T(8,128)(2,1)S(1)}, bf16[104,576]{1,0:T(8,128)(2,1)S(1)}, u32[]{:S(2)}, u32[]{:S(2)}) collective-permute-start(bf16[104,576]{1,0:T(8,128)(2,1)S(1)} %fusion.10), channel_id=1, source_target_pairs={{0,16},{2,18},{4,20},{6,22},{8,24},{10,26},{12,28},{14,30},{16,0},... | collective-permute-start | bytes 359432 | tf_op jit(solution)/shard_map/ppermute | solution.py:44
  269.8 7.1 %collective-permute-done.44 = bf16[2,120,768]{2,1,0:T(8,128)(2,1)S(1)} collective-permute-done((bf16[2,120,768]{2,1,0:T(8,128)(2,1)S(1)}, bf16[2,120,768]{2,1,0:T(8,128)(2,1)S(1)}, u32[]{:S(2)}, u32[]{:S(2)}) %collective-permute-start.44) | collective-permute-done | bytes 368672 | tf_op jit(solution)/shard_map/ppermute | solution.py:44
  277.1 3.0 collective-permute-start.45
  281.0 11.1 %collective-permute-done.45 = bf16[2,104,576]{2,1,0:T(8,128)(2,1)S(1)} collective-permute-done((bf16[2,104,576]{2,1,0:T(8,128)(2,1)S(1)}, bf16[2,104,576]{2,1,0:T(8,128)(2,1)S(1)}, u32[]{:S(2)}, u32[]{:S(2)}) %collective-permute-start.45) | collective-permute-done | bytes 239648 | tf_op jit(solution)/shard_map/ppermute | solution.py:44
  292.3 1.9 collective-permute-start.47
  295.2 2.0 collective-permute-start.49
  297.2 1.3 collective-permute-start.50
  298.5 8.6 %collective-permute-done.48.refs_15_ = bf16[384,256]{1,0:T(8,128)(2,1)} collective-permute-done((bf16[384,256]{1,0:T(8,128)(2,1)S(1)}, bf16[384,256]{1,0:T(8,128)(2,1)}, u32[]{:S(2)}, u32[]{:S(2)}) %collective-permute-start.48) | collective-permute-done | bytes 196640 | tf_op jit(solution)/shard_map/ppermute | solution.py:44
  307.7 6.0 %collective-permute-done.50.refs_17_ = bf16[384,256]{1,0:T(8,128)(2,1)S(1)} collective-permute-done((bf16[384,256]{1,0:T(8,128)(2,1)S(1)}, bf16[384,256]{1,0:T(8,128)(2,1)S(1)}, u32[]{:S(2)}, u32[]{:S(2)}) %collective-permute-start.50) | collective-permute-done | bytes 196640 | tf_op jit(solution)/shard_map/ppermute | solution.py:44
  314.2 2.2 collective-permute-start.54
  316.9 2.8 collective-permute-done.51.refs_7_
  320.9 10.4 %ending.1 = (f32[1536,768]{1,0:T(8,128)}, f32[384,3072]{1,0:T(8,128)}, f32[384,768]{1,0:T(8,128)}, f32[8,768]{1,0:T(8,128)}, f32[384,768]{1,0:T(8,128)}, /*index...) custom-call(s32[3]{0:T(128)} %get-tuple-element.202.scal.refs_0_.place, ...), custom_call_target="tpu_custom_call" | custom-call | flops 1 | bytes 1 | tf_op jit(solution)/shard_map/ending/pallas_call | solution.py:1293
  332.7 1.3 slice_reduce_fusion.2
  334.1 1.6 dynamic-slice_reduce_fusion
  (217 shorter events, 45.7 us)
Async XLA Ops:
  7.2 240.3 %reduce-scatter.2.cloned.1.call-start = ((), (), s32[]{:S(2)}) async-start(), calls=%async_computation.1 | async-start | bytes 1720320 | tf_op jit(solution)/shard_map/reduce_scatter | solution.py:1513
  7.2 24.1 %collective-permute-start.3 = (bf16[256,768]{1,0:T(8,128)(2,1)}, bf16[256,768]{1,0:T(8,128)(2,1)S(1)}, u32[]{:S(2)}, u32[]{:S(2)}) collective-permute-start(bf16[256,768]{1,0:T(8,128)(2,1)} %bitcast.70), channel_id=1, source_target_pairs={{0,16},{2,18},{4,20},{6,22},{8,24},{10,26},{12,28},{14,30},{16,0},... | collective-permute-start | bytes 1179656 | tf_op jit(solution)/shard_map/ppermute | solution.py:44
  10.4 20.9 %collective-permute-start.4 = (bf16[256,768]{1,0:T(8,128)(2,1)}, bf16[256,768]{1,0:T(8,128)(2,1)S(1)}, u32[]{:S(2)}, u32[]{:S(2)}) collective-permute-start(bf16[256,768]{1,0:T(8,128)(2,1)} %bitcast.71), channel_id=1, source_target_pairs={{0,8},{2,10},{4,12},{6,14},{8,0},{10,2},{12,4},{14,6},{16,24},{18,... | collective-permute-start | bytes 1179656 | tf_op jit(solution)/shard_map/ppermute | solution.py:44
  12.8 20.0 %copy-start.1 = (bf16[384,3072]{1,0:T(8,128)(2,1)S(1)}, bf16[384,3072]{1,0:T(8,128)(2,1)}, u32[]{:S(2)}) copy-start(bf16[384,3072]{1,0:T(8,128)(2,1)} %refs_12_.1) | copy-start | bytes 7077892
  18.4 6.5 %collective-permute-start.1 = (bf16[192,576]{1,0:T(8,128)(2,1)}, bf16[192,576]{1,0:T(8,128)(2,1)}, u32[]{:S(2)}, u32[]{:S(2)}) collective-permute-start(bf16[192,576]{1,0:T(8,128)(2,1)} %constant_dynamic-slice_fusion.5), channel_id=1, source_target_pairs={{0,1},{1,0},{2,3},{3,2},{4,5},{5,4},{6,7},{7,6},{8,9},{9,8},{10,11... | collective-permute-start | bytes 663560 | tf_op jit(solution)/shard_map/ppermute | solution.py:44
  20.7 10.6 %collective-permute-start = (bf16[192,768]{1,0:T(8,128)(2,1)S(1)}, bf16[192,768]{1,0:T(8,128)(2,1)}, u32[]{:S(2)}, u32[]{:S(2)}) collective-permute-start(bf16[192,768]{1,0:T(8,128)(2,1)S(1)} %constant_dynamic-slice_fusion.9), channel_id=1, source_target_pairs={{0,1},{1,0},{2,3},{3,2},{4,5},{5,4},{6,7},{7,6},{8,9},{9,8},{10,11... | collective-permute-start | bytes 884744 | tf_op jit(solution)/shard_map/ppermute | solution.py:44
  25.0 7.8 %collective-permute-start.2 = (bf16[192,576]{1,0:T(8,128)(2,1)}, bf16[192,576]{1,0:T(8,128)(2,1)}, u32[]{:S(2)}, u32[]{:S(2)}) collective-permute-start(bf16[192,576]{1,0:T(8,128)(2,1)} %collective-permute-done.1.mine), channel_id=1, source_target_pairs={{0,2},{2,0},{4,6},{6,4},{8,10},{10,8},{12,14},{14,12},{16,18},{18,... | collective-permute-start | bytes 663560 | tf_op jit(solution)/shard_map/ppermute | solution.py:44
  34.8 6.9 %collective-permute-start.7 = (bf16[48,3072]{1,0:T(8,128)(2,1)}, bf16[48,3072]{1,0:T(8,128)(2,1)S(1)}, u32[]{:S(2)}, u32[]{:S(2)}) collective-permute-start(bf16[48,3072]{1,0:T(8,128)(2,1)} %constant_dynamic-slice_fusion.1), channel_id=1, source_target_pairs={{0,1},{1,0},{2,3},{3,2},{4,5},{5,4},{6,7},{7,6},{8,9},{9,8},{10,11... | collective-permute-start | bytes 884744 | tf_op jit(solution)/shard_map/ppermute | solution.py:44
  36.1 8.4 %collective-permute-start.6 = (bf16[256,768]{1,0:T(8,128)(2,1)}, bf16[256,768]{1,0:T(8,128)(2,1)S(1)}, u32[]{:S(2)}, u32[]{:S(2)}) collective-permute-start(bf16[256,768]{1,0:T(8,128)(2,1)} %copy-done.11), channel_id=1, source_target_pairs={{0,8},{2,10},{4,12},{6,14},{8,0},{10,2},{12,4},{14,6},{16,24},{18,... | collective-permute-start | bytes 1179656 | tf_op jit(solution)/shard_map/ppermute | solution.py:44
  36.3 5.4 %collective-permute-start.5 = (bf16[12,384]{1,0:T(8,128)(2,1)S(1)}, bf16[12,384]{1,0:T(8,128)(2,1)S(1)}, u32[]{:S(2)}, u32[]{:S(2)}) collective-permute-start(bf16[12,384]{1,0:T(8,128)(2,1)S(1)} %copy-done.36), channel_id=1, source_target_pairs={{0,1},{1,0},{2,3},{3,2},{4,5},{5,4},{6,7},{7,6},{8,9},{9,8},{10,11... | collective-permute-start | bytes 27656 | tf_op jit(solution)/shard_map/ppermute | solution.py:44
  44.6 24.2 %collective-permute-start.10 = (bf16[144,3072]{1,0:T(8,128)(2,1)S(1)}, bf16[144,3072]{1,0:T(8,128)(2,1)S(1)}, u32[]{:S(2)}, u32[]{:S(2)}) collective-permute-start(bf16[144,3072]{1,0:T(8,128)(2,1)S(1)} %slice.86), channel_id=1, source_target_pairs={{0,1},{1,0},{2,3},{3,2},{4,5},{5,4},{6,7},{7,6},{8,9},{9,8},{10,11... | collective-permute-start | bytes 2654216 | tf_op jit(solution)/shard_map/ppermute | solution.py:44
  50.2 25.9 %copy-start.14 = (bf16[384,768]{1,0:T(8,128)(2,1)S(1)}, bf16[384,768]{1,0:T(8,128)(2,1)}, u32[]{:S(2)}) copy-start(bf16[384,768]{1,0:T(8,128)(2,1)} %param.19) | copy-start | bytes 1769476
  50.2 18.6 %collective-permute-start.9 = (bf16[384,1024]{1,0:T(8,128)(2,1)}, bf16[384,1024]{1,0:T(8,128)(2,1)S(1)}, u32[]{:S(2)}, u32[]{:S(2)}) collective-permute-start(bf16[384,1024]{1,0:T(8,128)(2,1)} %get-tuple-element.220.rest_0_.rest_4_), channel_id=1, source_target_pairs={{0,4},{2,6},{4,0},{6,2},{8,12},{10,14},{12,8},{14,10},{16,20},{18,... | collective-permute-start | bytes 2359304 | tf_op jit(solution)/shard_map/ppermute | solution.py:44
  51.5 5.2 %collective-permute-start.12 = (bf16[192,768]{1,0:T(8,128)(2,1)}, bf16[192,768]{1,0:T(8,128)(2,1)S(1)}, u32[]{:S(2)}, u32[]{:S(2)}) collective-permute-start(bf16[192,768]{1,0:T(8,128)(2,1)} %collective-permute-done.refs_10_), channel_id=1, source_target_pairs={{0,2},{2,0},{4,6},{6,4},{8,10},{10,8},{12,14},{14,12},{16,18},{18,... | collective-permute-start | bytes 884744 | tf_op jit(solution)/shard_map/ppermute | solution.py:44
  55.1 21.0 %copy-start.15 = (bf16[384,768]{1,0:T(8,128)(2,1)S(1)}, bf16[384,768]{1,0:T(8,128)(2,1)}, u32[]{:S(2)}) copy-start(bf16[384,768]{1,0:T(8,128)(2,1)} %param.21) | copy-start | bytes 1769476
  55.1 13.6 %collective-permute-start.11 = (bf16[192,768]{1,0:T(8,128)(2,1)S(1)}, bf16[192,768]{1,0:T(8,128)(2,1)S(1)}, u32[]{:S(2)}, u32[]{:S(2)}) collective-permute-start(bf16[192,768]{1,0:T(8,128)(2,1)S(1)} %slice.87), channel_id=1, source_target_pairs={{0,1},{1,0},{2,3},{3,2},{4,5},{5,4},{6,7},{7,6},{8,9},{9,8},{10,11... | collective-permute-start | bytes 884744 | tf_op jit(solution)/shard_map/ppermute | solution.py:44
  56.4 12.4 %collective-permute-start.13 = (bf16[48,3072]{1,0:T(8,128)(2,1)S(1)}, bf16[48,3072]{1,0:T(8,128)(2,1)S(1)}, u32[]{:S(2)}, u32[]{:S(2)}) collective-permute-start(bf16[48,3072]{1,0:T(8,128)(2,1)S(1)} %copy-done.29), channel_id=1, source_target_pairs={{0,2},{2,0},{4,6},{6,4},{8,10},{10,8},{12,14},{14,12},{16,18},{18,... | collective-permute-start | bytes 884744 | tf_op jit(solution)/shard_map/ppermute | solution.py:44
  56.7 18.7 %copy-start.30 = (bf16[192,768]{1,0:T(8,128)(2,1)}, bf16[192,768]{1,0:T(8,128)(2,1)S(1)}, u32[]{:S(2)}) copy-start(bf16[192,768]{1,0:T(8,128)(2,1)S(1)} %collective-permute-done.12.refs_11_) | copy-start | bytes 884740
  56.7 16.5 %collective-permute-start.8 = (bf16[384,1024]{1,0:T(8,128)(2,1)}, bf16[384,1024]{1,0:T(8,128)(2,1)S(1)}, u32[]{:S(2)}, u32[]{:S(2)}) collective-permute-start(bf16[384,1024]{1,0:T(8,128)(2,1)} %get-tuple-element.220.rest_0_.rest_4_), channel_id=1, source_target_pairs={{0,2},{2,0},{4,6},{6,4},{8,10},{10,8},{12,14},{14,12},{16,18},{18,... | collective-permute-start | bytes 2359304 | tf_op jit(solution)/shard_map/ppermute | solution.py:44
  68.8 6.3 %collective-permute-start.14 = (bf16[384,1024]{1,0:T(8,128)(2,1)S(1)}, bf16[384,1024]{1,0:T(8,128)(2,1)S(1)}, u32[]{:S(2)}, u32[]{:S(2)}) collective-permute-start(bf16[384,1024]{1,0:T(8,128)(2,1)S(1)} %collective-permute-done.9.rest_2_.rest_6_), channel_id=1, source_target_pairs={{0,2},{2,0},{4,6},{6,4},{8,10},{10,8},{12,14},{14,12},{16,18},{18,... | collective-permute-start | bytes 2359304 | tf_op jit(solution)/shard_map/ppermute | solution.py:44
  75.1 20.9 %collective-permute-start.15 = (bf16[576,768]{1,0:T(8,128)(2,1)S(1)}, bf16[576,768]{1,0:T(8,128)(2,1)S(1)}, u32[]{:S(2)}, u32[]{:S(2)}) collective-permute-start(bf16[576,768]{1,0:T(8,128)(2,1)S(1)} %slice.88), channel_id=1, source_target_pairs={{0,1},{1,0},{2,3},{3,2},{4,5},{5,4},{6,7},{7,6},{8,9},{9,8},{10,11... | collective-permute-start | bytes 2654216 | tf_op jit(solution)/shard_map/ppermute | solution.py:44
  75.4 20.6 %collective-permute-start.16 = (bf16[144,3072]{1,0:T(8,128)(2,1)S(1)}, bf16[144,3072]{1,0:T(8,128)(2,1)S(1)}, u32[]{:S(2)}, u32[]{:S(2)}) collective-permute-start(bf16[144,3072]{1,0:T(8,128)(2,1)S(1)} %collective-permute-done.10.refs_14_), channel_id=1, source_target_pairs={{0,2},{2,0},{4,6},{6,4},{8,10},{10,8},{12,14},{14,12},{16,18},{18,... | collective-permute-start | bytes 2654216 | tf_op jit(solution)/shard_map/ppermute | solution.py:44
  76.5 18.6 %collective-permute-start.17 = (bf16[192,768]{1,0:T(8,128)(2,1)S(1)}, bf16[192,768]{1,0:T(8,128)(2,1)S(1)}, u32[]{:S(2)}, u32[]{:S(2)}) collective-permute-start(bf16[192,768]{1,0:T(8,128)(2,1)S(1)} %collective-permute-done.11.refs_18_), channel_id=1, source_target_pairs={{0,2},{2,0},{4,6},{6,4},{8,10},{10,8},{12,14},{14,12},{16,18},{18,... | collective-permute-start | bytes 884744 | tf_op jit(solution)/shard_map/ppermute | solution.py:44
  96.1 10.9 %collective-permute-start.21 = (bf16[576,768]{1,0:T(8,128)(2,1)S(1)}, bf16[576,768]{1,0:T(8,128)(2,1)S(1)}, u32[]{:S(2)}, u32[]{:S(2)}) collective-permute-start(bf16[576,768]{1,0:T(8,128)(2,1)S(1)} %collective-permute-done.15.refs_19_), channel_id=1, source_target_pairs={{0,2},{2,0},{4,6},{6,4},{8,10},{10,8},{12,14},{14,12},{16,18},{18,... | collective-permute-start | bytes 2654216 | tf_op jit(solution)/shard_map/ppermute | solution.py:44
  97.3 5.7 %collective-permute-start.18 = (bf16[192,256]{1,0:T(8,128)(2,1)}, bf16[192,256]{1,0:T(8,128)(2,1)S(1)}, u32[]{:S(2)}, u32[]{:S(2)}) collective-permute-start(bf16[192,256]{1,0:T(8,128)(2,1)} %get-tuple-element.236), channel_id=1, source_target_pairs={{0,8},{2,10},{4,12},{6,14},{8,0},{10,2},{12,4},{14,6},{16,24},{18,... | collective-permute-start | bytes 294920 | tf_op jit(solution)/shard_map/ppermute | solution.py:44
  97.5 9.4 %collective-permute-start.19 = (bf16[192,256]{1,0:T(8,128)(2,1)}, bf16[192,256]{1,0:T(8,128)(2,1)S(1)}, u32[]{:S(2)}, u32[]{:S(2)}) collective-permute-start(bf16[192,256]{1,0:T(8,128)(2,1)} %get-tuple-element.237), channel_id=1, source_target_pairs={{0,16},{2,18},{4,20},{6,22},{8,24},{10,26},{12,28},{14,30},{16,0},... | collective-permute-start | bytes 294920 | tf_op jit(solution)/shard_map/ppermute | solution.py:44
  99.0 7.9 %collective-permute-start.20 = (bf16[192,256]{1,0:T(8,128)(2,1)}, bf16[192,256]{1,0:T(8,128)(2,1)S(1)}, u32[]{:S(2)}, u32[]{:S(2)}) collective-permute-start(bf16[192,256]{1,0:T(8,128)(2,1)} %get-tuple-element.238), channel_id=1, source_target_pairs={{0,24},{2,26},{4,28},{6,30},{8,16},{10,18},{12,20},{14,22},{16,8},... | collective-permute-start | bytes 294920 | tf_op jit(solution)/shard_map/ppermute | solution.py:44
  107.0 23.5 %collective-permute-start.22 = (bf16[192,2304]{1,0:T(8,128)(2,1)S(1)}, bf16[192,2304]{1,0:T(8,128)(2,1)S(1)}, u32[]{:S(2)}, u32[]{:S(2)}) collective-permute-start(bf16[192,2304]{1,0:T(8,128)(2,1)S(1)} %constant_dynamic-slice_fusion.2), channel_id=1, source_target_pairs={{0,1},{1,0},{2,3},{3,2},{4,5},{5,4},{6,7},{7,6},{8,9},{9,8},{10,11... | collective-permute-start | bytes 2654216 | tf_op jit(solution)/shard_map/ppermute | solution.py:44
  130.4 14.1 %collective-permute-start.26 = (bf16[2,960,768]{2,1,0:T(8,128)(2,1)}, bf16[2,960,768]{2,1,0:T(8,128)(2,1)}, u32[]{:S(2)}, u32[]{:S(2)}) collective-permute-start(bf16[2,960,768]{2,1,0:T(8,128)(2,1)} %get-tuple-element.270), channel_id=1, source_target_pairs={{0,2},{2,0},{4,6},{6,4},{8,10},{10,8},{12,14},{14,12},{16,18},{18,... | collective-permute-start | bytes 8847368 | tf_op jit(solution)/shard_map/ppermute | solution.py:44
  132.4 9.0 %collective-permute-start.27 = (bf16[2,832,768]{2,1,0:T(8,128)(2,1)}, bf16[2,832,768]{2,1,0:T(8,128)(2,1)}, u32[]{:S(2)}, u32[]{:S(2)}) collective-permute-start(bf16[2,832,768]{2,1,0:T(8,128)(2,1)} %get-tuple-element.273), channel_id=1, source_target_pairs={{0,2},{2,0},{4,6},{6,4},{8,10},{10,8},{12,14},{14,12},{16,18},{18,... | collective-permute-start | bytes 7667720 | tf_op jit(solution)/shard_map/ppermute | solution.py:44
  132.5 14.8 %collective-permute-start.23 = (bf16[192,256]{1,0:T(8,128)(2,1)}, bf16[192,256]{1,0:T(8,128)(2,1)S(1)}, u32[]{:S(2)}, u32[]{:S(2)}) collective-permute-start(bf16[192,256]{1,0:T(8,128)(2,1)} %get-tuple-element.266), channel_id=1, source_target_pairs={{0,8},{2,10},{4,12},{6,14},{8,0},{10,2},{12,4},{14,6},{16,24},{18,... | collective-permute-start | bytes 294920 | tf_op jit(solution)/shard_map/ppermute | solution.py:44
  134.1 13.2 %collective-permute-start.24 = (bf16[192,256]{1,0:T(8,128)(2,1)}, bf16[192,256]{1,0:T(8,128)(2,1)S(1)}, u32[]{:S(2)}, u32[]{:S(2)}) collective-permute-start(bf16[192,256]{1,0:T(8,128)(2,1)} %get-tuple-element.267), channel_id=1, source_target_pairs={{0,16},{2,18},{4,20},{6,22},{8,24},{10,26},{12,28},{14,30},{16,0},... | collective-permute-start | bytes 294920 | tf_op jit(solution)/shard_map/ppermute | solution.py:44
  134.2 13.2 %collective-permute-start.25 = (bf16[192,256]{1,0:T(8,128)(2,1)}, bf16[192,256]{1,0:T(8,128)(2,1)S(1)}, u32[]{:S(2)}, u32[]{:S(2)}) collective-permute-start(bf16[192,256]{1,0:T(8,128)(2,1)} %get-tuple-element.268), channel_id=1, source_target_pairs={{0,24},{2,26},{4,28},{6,30},{8,16},{10,18},{12,20},{14,22},{16,8},... | collective-permute-start | bytes 294920 | tf_op jit(solution)/shard_map/ppermute | solution.py:44
  147.4 33.9 %collective-permute-start.28 = (bf16[960,768]{1,0:T(8,128)(2,1)}, bf16[960,768]{1,0:T(8,128)(2,1)}, u32[]{:S(2)}, u32[]{:S(2)}) collective-permute-start(bf16[960,768]{1,0:T(8,128)(2,1)} %fusion), channel_id=1, source_target_pairs={{0,1},{1,0},{2,3},{3,2},{4,5},{5,4},{6,7},{7,6},{8,9},{9,8},{10,11... | collective-permute-start | bytes 4423688 | tf_op jit(solution)/shard_map/ppermute | solution.py:44
  148.4 29.3 %collective-permute-start.29 = (bf16[2,416,768]{2,1,0:T(8,128)(2,1)}, bf16[2,416,768]{2,1,0:T(8,128)(2,1)}, u32[]{:S(2)}, u32[]{:S(2)}) collective-permute-start(bf16[2,416,768]{2,1,0:T(8,128)(2,1)} %add_convert_fusion.1), channel_id=1, source_target_pairs={{0,4},{2,6},{4,0},{6,2},{8,12},{10,14},{12,8},{14,10},{16,20},{18,... | collective-permute-start | bytes 3833864 | tf_op jit(solution)/shard_map/ppermute | solution.py:44
  149.6 40.4 %collective-permute-start.34 = (bf16[192,2304]{1,0:T(8,128)(2,1)}, bf16[192,2304]{1,0:T(8,128)(2,1)}, u32[]{:S(2)}, u32[]{:S(2)}) collective-permute-start(bf16[192,2304]{1,0:T(8,128)(2,1)} %copy-done.17), channel_id=1, source_target_pairs={{0,2},{2,0},{4,6},{6,4},{8,10},{10,8},{12,14},{14,12},{16,18},{18,... | collective-permute-start | bytes 2654216 | tf_op jit(solution)/shard_map/ppermute | solution.py:44
  181.3 23.2 %collective-permute-start.32 = (bf16[384,1024]{1,0:T(8,128)(2,1)}, bf16[384,1024]{1,0:T(8,128)(2,1)}, u32[]{:S(2)}, u32[]{:S(2)}) collective-permute-start(bf16[384,1024]{1,0:T(8,128)(2,1)} %get-tuple-element.291), channel_id=1, source_target_pairs={{0,2},{2,0},{4,6},{6,4},{8,10},{10,8},{12,14},{14,12},{16,18},{18,... | collective-permute-start | bytes 2359304 | tf_op jit(solution)/shard_map/ppermute | solution.py:44
  182.5 22.0 %collective-permute-start.33 = (bf16[384,1024]{1,0:T(8,128)(2,1)}, bf16[384,1024]{1,0:T(8,128)(2,1)}, u32[]{:S(2)}, u32[]{:S(2)}) collective-permute-start(bf16[384,1024]{1,0:T(8,128)(2,1)} %get-tuple-element.292), channel_id=1, source_target_pairs={{0,2},{2,0},{4,6},{6,4},{8,10},{10,8},{12,14},{14,12},{16,18},{18,... | collective-permute-start | bytes 2359304 | tf_op jit(solution)/shard_map/ppermute | solution.py:44
  185.1 19.4 %collective-permute-start.30 = (bf16[480,768]{1,0:T(8,128)(2,1)}, bf16[480,768]{1,0:T(8,128)(2,1)}, u32[]{:S(2)}, u32[]{:S(2)}) collective-permute-start(bf16[480,768]{1,0:T(8,128)(2,1)} %fusion.3), channel_id=1, source_target_pairs={{0,4},{2,6},{4,0},{6,2},{8,12},{10,14},{12,8},{14,10},{16,20},{18,... | collective-permute-start | bytes 2211848 | tf_op jit(solution)/shard_map/ppermute | solution.py:44
  189.1 15.4 %collective-permute-start.31 = (bf16[416,768]{1,0:T(8,128)(2,1)}, bf16[416,768]{1,0:T(8,128)(2,1)}, u32[]{:S(2)}, u32[]{:S(2)}) collective-permute-start(bf16[416,768]{1,0:T(8,128)(2,1)} %fusion.5), channel_id=1, source_target_pairs={{0,1},{1,0},{2,3},{3,2},{4,5},{5,4},{6,7},{7,6},{8,9},{9,8},{10,11... | collective-permute-start | bytes 1916936 | tf_op jit(solution)/shard_map/ppermute | solution.py:44
  210.0 110.1 %all-gather.3.cloned.1.call-start = ((), (), s32[]{:S(2)}) async-start(), calls=%async_computation.2 | async-start | bytes 2715648 | tf_op jit(solution)/shard_map/all_gather | solution.py:1532
  211.7 17.5 %collective-permute-start.35 = (bf16[384,1024]{1,0:T(8,128)(2,1)S(1)}, bf16[384,1024]{1,0:T(8,128)(2,1)S(1)}, u32[]{:S(2)}, u32[]{:S(2)}) collective-permute-start(bf16[384,1024]{1,0:T(8,128)(2,1)S(1)} %add_convert_fusion.3), channel_id=1, source_target_pairs={{0,4},{2,6},{4,0},{6,2},{8,12},{10,14},{12,8},{14,10},{16,20},{18,... | collective-permute-start | bytes 2359304 | tf_op jit(solution)/shard_map/ppermute | solution.py:44
  212.6 7.0 %collective-permute-start.36 = (bf16[192,256]{1,0:T(8,128)(2,1)S(1)}, bf16[192,256]{1,0:T(8,128)(2,1)S(1)}, u32[]{:S(2)}, u32[]{:S(2)}) collective-permute-start(bf16[192,256]{1,0:T(8,128)(2,1)S(1)} %get-tuple-element.306), channel_id=1, source_target_pairs={{0,8},{2,10},{4,12},{6,14},{8,0},{10,2},{12,4},{14,6},{16,24},{18,... | collective-permute-start | bytes 294920 | tf_op jit(solution)/shard_map/ppermute | solution.py:44
  214.2 14.2 %collective-permute-start.37 = (bf16[192,256]{1,0:T(8,128)(2,1)S(1)}, bf16[192,256]{1,0:T(8,128)(2,1)S(1)}, u32[]{:S(2)}, u32[]{:S(2)}) collective-permute-start(bf16[192,256]{1,0:T(8,128)(2,1)S(1)} %get-tuple-element.307), channel_id=1, source_target_pairs={{0,16},{2,18},{4,20},{6,22},{8,24},{10,26},{12,28},{14,30},{16,0},... | collective-permute-start | bytes 294920 | tf_op jit(solution)/shard_map/ppermute | solution.py:44
  214.2 14.2 %collective-permute-start.38 = (bf16[192,256]{1,0:T(8,128)(2,1)S(1)}, bf16[192,256]{1,0:T(8,128)(2,1)S(1)}, u32[]{:S(2)}, u32[]{:S(2)}) collective-permute-start(bf16[192,256]{1,0:T(8,128)(2,1)S(1)} %get-tuple-element.308), channel_id=1, source_target_pairs={{0,24},{2,26},{4,28},{6,30},{8,16},{10,18},{12,20},{14,22},{16,8},... | collective-permute-start | bytes 294920 | tf_op jit(solution)/shard_map/ppermute | solution.py:44
  236.3 19.5 %copy-start.27 = (bf16[2,208,576]{2,1,0:T(8,128)(2,1)S(1)}, bf16[2,208,576]{2,1,0:T(8,128)(2,1)}, u32[]{:S(2)}) copy-start(bf16[2,208,576]{2,1,0:T(8,128)(2,1)} %get-tuple-element.314) | copy-start | bytes 1437700
  236.3 4.3 %collective-permute-start.39 = (bf16[2,208,576]{2,1,0:T(8,128)(2,1)}, bf16[2,208,576]{2,1,0:T(8,128)(2,1)S(1)}, u32[]{:S(2)}, u32[]{:S(2)}) collective-permute-start(bf16[2,208,576]{2,1,0:T(8,128)(2,1)} %get-tuple-element.315), channel_id=1, source_target_pairs={{0,2},{2,0},{4,6},{6,4},{8,10},{10,8},{12,14},{14,12},{16,18},{18,... | collective-permute-start | bytes 1437704 | tf_op jit(solution)/shard_map/ppermute | solution.py:44
  249.1 6.7 %collective-permute-start.40 = (bf16[208,576]{1,0:T(8,128)(2,1)S(1)}, bf16[208,576]{1,0:T(8,128)(2,1)S(1)}, u32[]{:S(2)}, u32[]{:S(2)}) collective-permute-start(bf16[208,576]{1,0:T(8,128)(2,1)S(1)} %fusion.7), channel_id=1, source_target_pairs={{0,1},{1,0},{2,3},{3,2},{4,5},{5,4},{6,7},{7,6},{8,9},{9,8},{10,11... | collective-permute-start | bytes 718856 | tf_op jit(solution)/shard_map/ppermute | solution.py:44
  251.0 9.3 %collective-permute-start.42 = (bf16[120,768]{1,0:T(8,128)(2,1)S(1)}, bf16[120,768]{1,0:T(8,128)(2,1)S(1)}, u32[]{:S(2)}, u32[]{:S(2)}) collective-permute-start(bf16[120,768]{1,0:T(8,128)(2,1)S(1)} %get-tuple-element.404), channel_id=1, source_target_pairs={{0,16},{2,18},{4,20},{6,22},{8,24},{10,26},{12,28},{14,30},{16,0},... | collective-permute-start | bytes 552968 | tf_op jit(solution)/shard_map/ppermute | solution.py:44
  260.4 16.5 %collective-permute-start.44 = (bf16[2,120,768]{2,1,0:T(8,128)(2,1)S(1)}, bf16[2,120,768]{2,1,0:T(8,128)(2,1)S(1)}, u32[]{:S(2)}, u32[]{:S(2)}) collective-permute-start(bf16[2,120,768]{2,1,0:T(8,128)(2,1)S(1)} %pad_maximum_fusion.3), channel_id=1, source_target_pairs={{0,8},{2,10},{4,12},{6,14},{8,0},{10,2},{12,4},{14,6},{16,24},{18,... | collective-permute-start | bytes 1105928 | tf_op jit(solution)/shard_map/ppermute | solution.py:44
  261.2 3.8 %collective-permute-start.41 = (bf16[104,576]{1,0:T(8,128)(2,1)S(1)}, bf16[104,576]{1,0:T(8,128)(2,1)S(1)}, u32[]{:S(2)}, u32[]{:S(2)}) collective-permute-start(bf16[104,576]{1,0:T(8,128)(2,1)S(1)} %fusion.8), channel_id=1, source_target_pairs={{0,4},{2,6},{4,0},{6,2},{8,12},{10,14},{12,8},{14,10},{16,20},{18,... | collective-permute-start | bytes 359432 | tf_op jit(solution)/shard_map/ppermute | solution.py:44
  265.2 11.8 %collective-permute-start.43 = (bf16[104,576]{1,0:T(8,128)(2,1)S(1)}, bf16[104,576]{1,0:T(8,128)(2,1)S(1)}, u32[]{:S(2)}, u32[]{:S(2)}) collective-permute-start(bf16[104,576]{1,0:T(8,128)(2,1)S(1)} %fusion.10), channel_id=1, source_target_pairs={{0,16},{2,18},{4,20},{6,22},{8,24},{10,26},{12,28},{14,30},{16,0},... | collective-permute-start | bytes 359432 | tf_op jit(solution)/shard_map/ppermute | solution.py:44
  277.0 30.1 %copy-start.8 = (bf16[2,2,120,768]{3,2,1,0:T(8,128)(2,1)}, bf16[2,2,120,768]{3,2,1,0:T(8,128)(2,1)S(1)}, u32[]{:S(2)}) copy-start(bf16[2,2,120,768]{3,2,1,0:T(8,128)(2,1)S(1)} %pad_maximum_fusion.1) | copy-start | bytes 2211844
  277.1 15.0 %collective-permute-start.45 = (bf16[2,104,576]{2,1,0:T(8,128)(2,1)S(1)}, bf16[2,104,576]{2,1,0:T(8,128)(2,1)S(1)}, u32[]{:S(2)}, u32[]{:S(2)}) collective-permute-start(bf16[2,104,576]{2,1,0:T(8,128)(2,1)S(1)} %maximum_select_fusion.1), channel_id=1, source_target_pairs={{0,8},{2,10},{4,12},{6,14},{8,0},{10,2},{12,4},{14,6},{16,24},{18,... | collective-permute-start | bytes 718856 | tf_op jit(solution)/shard_map/ppermute | solution.py:44
  280.1 34.1 %collective-permute-start.46 = (bf16[2,2,120,768]{3,2,1,0:T(8,128)(2,1)S(1)}, bf16[2,2,120,768]{3,2,1,0:T(8,128)(2,1)S(1)}, u32[]{:S(2)}, u32[]{:S(2)}) collective-permute-start(bf16[2,2,120,768]{3,2,1,0:T(8,128)(2,1)S(1)} %pad_maximum_fusion.1), channel_id=1, source_target_pairs={{0,4},{2,6},{4,0},{6,2},{8,12},{10,14},{12,8},{14,10},{16,20},{18,... | collective-permute-start | bytes 2211848 | tf_op jit(solution)/shard_map/ppermute | solution.py:44
  292.3 27.8 %copy-start.9 = (bf16[2,2,104,576]{3,2,1,0:T(8,128)(2,1)}, bf16[2,2,104,576]{3,2,1,0:T(8,128)(2,1)S(1)}, u32[]{:S(2)}) copy-start(bf16[2,2,104,576]{3,2,1,0:T(8,128)(2,1)S(1)} %copy.42) | copy-start | bytes 1437700
  292.3 21.9 %collective-permute-start.47 = (bf16[4,104,576]{2,1,0:T(8,128)(2,1)S(1)}, bf16[4,104,576]{2,1,0:T(8,128)(2,1)}, u32[]{:S(2)}, u32[]{:S(2)}) collective-permute-start(bf16[4,104,576]{2,1,0:T(8,128)(2,1)S(1)} %bitcast.79), channel_id=1, source_target_pairs={{0,4},{2,6},{4,0},{6,2},{8,12},{10,14},{12,8},{14,10},{16,20},{18,... | collective-permute-start | bytes 1437704 | tf_op jit(solution)/shard_map/ppermute | solution.py:44
  295.0 12.1 %collective-permute-start.48 = (bf16[384,256]{1,0:T(8,128)(2,1)S(1)}, bf16[384,256]{1,0:T(8,128)(2,1)}, u32[]{:S(2)}, u32[]{:S(2)}) collective-permute-start(bf16[384,256]{1,0:T(8,128)(2,1)S(1)} %get-tuple-element.329), channel_id=1, source_target_pairs={{0,8},{2,10},{4,12},{6,14},{8,0},{10,2},{12,4},{14,6},{16,24},{18,... | collective-permute-start | bytes 589832 | tf_op jit(solution)/shard_map/ppermute | solution.py:44
  295.2 12.5 %collective-permute-start.49 = (bf16[384,256]{1,0:T(8,128)(2,1)S(1)}, bf16[384,256]{1,0:T(8,128)(2,1)S(1)}, u32[]{:S(2)}, u32[]{:S(2)}) collective-permute-start(bf16[384,256]{1,0:T(8,128)(2,1)S(1)} %get-tuple-element.330), channel_id=1, source_target_pairs={{0,16},{2,18},{4,20},{6,22},{8,24},{10,26},{12,28},{14,30},{16,0},... | collective-permute-start | bytes 589832 | tf_op jit(solution)/shard_map/ppermute | solution.py:44
  297.2 16.5 %collective-permute-start.50 = (bf16[384,256]{1,0:T(8,128)(2,1)S(1)}, bf16[384,256]{1,0:T(8,128)(2,1)S(1)}, u32[]{:S(2)}, u32[]{:S(2)}) collective-permute-start(bf16[384,256]{1,0:T(8,128)(2,1)S(1)} %get-tuple-element.331), channel_id=1, source_target_pairs={{0,24},{2,26},{4,28},{6,30},{8,16},{10,18},{12,20},{14,22},{16,8},... | collective-permute-start | bytes 589832 | tf_op jit(solution)/shard_map/ppermute | solution.py:44
  307.1 12.6 %collective-permute-start.53 = (bf16[2,2,120,768]{3,2,1,0:T(8,128)(2,1)S(1)}, bf16[2,2,120,768]{3,2,1,0:T(8,128)(2,1)S(1)}, u32[]{:S(2)}, u32[]{:S(2)}) collective-permute-start(bf16[2,2,120,768]{3,2,1,0:T(8,128)(2,1)S(1)} %pad_maximum_fusion.1), channel_id=1, source_target_pairs={{0,2},{2,0},{4,6},{6,4},{8,10},{10,8},{12,14},{14,12},{16,18},{18,... | collective-permute-start | bytes 2211848 | tf_op jit(solution)/shard_map/ppermute | solution.py:44
  314.2 5.9 %collective-permute-start.54 = (bf16[2,2,120,768]{3,2,1,0:T(8,128)(2,1)S(1)}, bf16[2,2,120,768]{3,2,1,0:T(8,128)(2,1)S(1)}, u32[]{:S(2)}, u32[]{:S(2)}) collective-permute-start(bf16[2,2,120,768]{3,2,1,0:T(8,128)(2,1)S(1)} %collective-permute-done.46), channel_id=1, source_target_pairs={{0,2},{2,0},{4,6},{6,4},{8,10},{10,8},{12,14},{14,12},{16,18},{18,... | collective-permute-start | bytes 2211848 | tf_op jit(solution)/shard_map/ppermute | solution.py:44
  316.4 3.4 collective-permute-start.51
  316.4 3.6 %collective-permute-start.52 = (bf16[4,104,576]{2,1,0:T(8,128)(2,1)}, bf16[4,104,576]{2,1,0:T(8,128)(2,1)}, u32[]{:S(2)}, u32[]{:S(2)}) collective-permute-start(bf16[4,104,576]{2,1,0:T(8,128)(2,1)} %collective-permute-done.47.refs_6_), channel_id=1, source_target_pairs={{0,2},{2,0},{4,6},{6,4},{8,10},{10,8},{12,14},{14,12},{16,18},{18,... | collective-permute-start | bytes 1437704 | tf_op jit(solution)/shard_map/ppermute | solution.py:44
  (43 other events, 245.2 us)
Sparse Core Ops, SparseCore 0:
  210.1 37.2 reduce-scatter.1
  250.4 54.0 all-gather.2
where the time goes:
time: 344 us; the launch traced here: 343 us
  waiting for transfers between devices  121 us (35%)
  Pallas kernels  88.1 us (26%)
  starting transfers between devices  70.4 us (20%)
  other arithmetic  25.8 us (8%)
  local copies, waits for them, and re-layouts  22.5 us (7%)
  between operations  14.6 us (4%)
    ppermute x55, waiting for transfers between devices, swap(): return lax.ppermute(v, axis, [(i, i ^ bit) for i in range(n)])  115 us
    ppermute x55, starting transfers between devices, swap(): return lax.ppermute(v, axis, [(i, i ^ bit) for i in range(n)])  70.4 us
    pallas_call x1, Pallas kernels, group_bwd(): pl.pallas_call(functools.partial(group_bwd_kernel, members, block), out_s...  22.8 us
    pallas_call x1, Pallas kernels, middle(): pl.pallas_call(functools.partial(middle_kernel, block), out_shape=(jax.Sh...  22.5 us
    pallas_call x1, Pallas kernels, group_fwd(): pl.pallas_call(functools.partial(group_fwd_kernel, members, block), out_s...  18.1 us
    convert_element_type x9, other arithmetic, low_sum(): return then(sum((cut(t).astype(f32) for t in terms)).astype(bf16))  16.4 us
    pallas_call x1, Pallas kernels, ending(): pl.pallas_call(ending_kernel, out_shape=tuple((jax.ShapeDtypeStruct(s, f3...  10.4 us
  transfers between devices with their start and end apart: 57, of which 27 were waited for; matrix products, arithmetic and copies ran while one was open for 9% of the time, Pallas kernels for 23%

commit v1 on v0

--- a/solution.py
+++ b/solution.py
@@ -490,6 +490,7 @@
 CHEAP = pl.CostEstimate(flops=1, transcendentals=0, bytes_accessed=1)
 EXTRA = 8
 SPARE = 64
+OUT_A = 128
 SMEM = pl.BlockSpec(memory_space=pltpu.SMEM)
 
 
@@ -1000,13 +1001,13 @@
 
         @pl.when(core == 0)
         def _(y=y, spare=spare, none=none):
-            keeps[0][y, 4 * quarter :] = spare
-            sends[0][y, 4 * quarter :] = none
+            keeps[0][y, 4 * quarter : 4 * quarter + SPARE] = spare
+            sends[0][y, 4 * quarter : 4 * quarter + SPARE] = none
 
         @pl.when(core != 0)
         def _(y=y, spare=spare, none=none):
-            keeps[0][y, 4 * quarter :] = none
-            sends[0][y, 4 * quarter :] = spare
+            keeps[0][y, 4 * quarter : 4 * quarter + SPARE] = none
+            sends[0][y, 4 * quarter : 4 * quarter + SPARE] = spare
 
     dot_scr[...] = dot(wout[...], dab, 1, 1).astype(bf16)
     for j in range(NG):
@@ -1019,11 +1020,13 @@
 
             @pl.when(core == c)
             def _(piece=piece, y=y):
-                keeps[1][y, ffq:] = piece
+                keeps[1][y, ffq:] = piece[:OUT_A]
+                keeps[0][y, 4 * quarter + SPARE :] = piece[OUT_A:]
 
             @pl.when(core != c)
             def _(piece=piece, y=y):
-                sends[1][y, ffq:] = piece
+                sends[1][y, ffq:] = piece[:OUT_A]
+                sends[0][y, 4 * quarter + SPARE :] = piece[OUT_A:]
 
     store(lambda n: (ffq, n))
     for c in stored:
@@ -1035,8 +1038,8 @@
     ffq = inners[0].shape[1] // 4
     q = width // 4
     grads = [
-        jax.ShapeDtypeStruct((2, 4 * q + SPARE, ffq), bf16),
-        jax.ShapeDtypeStruct((2, ffq + q, width), bf16),
+        jax.ShapeDtypeStruct((2, 5 * q + SPARE - OUT_A, ffq), bf16),
+        jax.ShapeDtypeStruct((2, ffq + OUT_A, width), bf16),
     ]
     return pl.pallas_call(
         functools.partial(middle_kernel, block),
@@ -1208,7 +1211,7 @@
         for g in range(NG):
             j = jnp.bitwise_xor(g_id, g)
             v = parts_a[s, jnp.bitwise_and(j, 1) * 2 + jnp.right_shift(j, 1)].astype(f32)
-            spread_rows(((ffq, outer), (quarter, out)), (NG * x + g) * n_a, v)
+            spread_rows(((ffq, outer), (OUT_A, out)), (NG * x + g) * n_a, v)
 
     each_part(scal, put_a)
     for i in range(whole_b.shape[0]):
@@ -1217,12 +1220,17 @@
             at = c * quarter + row
             inner_ref[at : at + v.shape[0], a * ffq : (a + 1) * ffq] = v
 
+        def out(row, v, c=c):
+            at = c * quarter + OUT_A + row
+            out_ref[at : at + v.shape[0], :] = v
+
         def sums(row, v, c=c):
             if c == 0 and row < 8:
                 vec_ref[row : min(8, row + v.shape[0]), :] = v[: 8 - row]
 
         spread_rows(
-            tuple((quarter, functools.partial(inner, a)) for a in range(4)) + ((SPARE, sums),),
+            tuple((quarter, functools.partial(inner, a)) for a in range(4))
+            + ((SPARE, sums), (quarter - OUT_A, out)),
             (NG * x + g) * n_b,
             whole_b[i].astype(f32),
         )

time: 344 us -> 338 us (0.983)
  starting transfers between devices: 70.4 us -> 79.4 us
  Pallas kernels: 88.1 us -> 80.4 us
  other arithmetic: 25.8 us -> 21.1 us
    ppermute x55, starting transfers between devices: 70.4 us -> 79.3 us  [swap(): return lax.ppermute(v, axis, [(i, i ^ bit) for i in range(n)])]
    ppermute x55, waiting for transfers between devices: 115 us -> 110 us  [swap(): return lax.ppermute(v, axis, [(i, i ^ bit) for i in range(n)])]
    pallas_call x1, Pallas kernels: 22.8 us -> 18.4 us  [group_bwd(): pl.pallas_call(functools.partial(group_bwd_kernel, members, block), out_s...]
    convert_element_type x9, other arithmetic: 16.4 us -> 12.2 us  [low_sum(): return then(sum((cut(t).astype(f32) for t in terms)).astype(bf16))]
  transfers between devices with their start and end apart: 57 -> 57, of which waited for: 27 -> 27; matrix products, arithmetic and copies ran while one was open for 9% -> 7% of each run, Pallas kernels for 23% -> 21%
where the time goes in v1:
time: 338 us; the launch traced here: 336 us
  waiting for transfers between devices  118 us (35%)
  Pallas kernels  80.4 us (24%)
  starting transfers between devices  79.4 us (23%)
  local copies, waits for them, and re-layouts  23 us (7%)
  other arithmetic  21.1 us (6%)
  between operations  14.7 us (4%)
    ppermute x55, waiting for transfers between devices, swap(): return lax.ppermute(v, axis, [(i, i ^ bit) for i in range(n)])  110 us
    ppermute x55, starting transfers between devices, swap(): return lax.ppermute(v, axis, [(i, i ^ bit) for i in range(n)])  79.3 us
    pallas_call x1, Pallas kernels, middle(): pl.pallas_call(functools.partial(middle_kernel, block), out_shape=(jax.Sh...  22.5 us
    pallas_call x1, Pallas kernels, group_bwd(): pl.pallas_call(functools.partial(group_bwd_kernel, members, block), out_s...  18.4 us
    pallas_call x1, Pallas kernels, group_fwd(): pl.pallas_call(functools.partial(group_fwd_kernel, members, block), out_s...  14.7 us
    convert_element_type x9, other arithmetic, low_sum(): return then(sum((cut(t).astype(f32) for t in terms)).astype(bf16))  12.2 us
    pallas_call x1, Pallas kernels, ending(): pl.pallas_call(ending_kernel, out_shape=tuple((jax.ShapeDtypeStruct(s, f3...  10.4 us
    reduce_scatter x1, waiting for transfers between devices, fast_device(): lax.psum_scatter(chunk, 'ctx', scatter_dimension=0, tiled=True, axis_inde...  7.98 us
  transfers between devices with their start and end apart: 57, of which 27 were waited for; matrix products, arithmetic and copies ran while one was open for 7% of the time, Pallas kernels for 21%

profile of v1, /device:TPU:1, one launch (start us, length us, event | category | flops | bytes accessed | tf_op | source)
XLA Modules:
  0.0 336.3 jit_solution(6582769222195641396)
XLA Ops:
  7.2 3.2 collective-permute-start.3
  10.4 1.3 collective-permute-start.4
  14.1 1.8 constant_dynamic-slice_fusion.8
  21.7 1.4 pack.1.small.refs_7_
  23.2 1.8 collective-permute-done.1.mine
  25.0 3.9 %collective-permute-start.2 = (bf16[192,576]{1,0:T(8,128)(2,1)}, bf16[192,576]{1,0:T(8,128)(2,1)}, u32[]{:S(2)}, u32[]{:S(2)}) collective-permute-start(bf16[192,576]{1,0:T(8,128)(2,1)} %collective-permute-done.1.mine), channel_id=1, source_target_pairs={{0,2},{2,0},{4,6},{6,4},{8,10},{10,8},{12,14},{14,12},{16,18},{18,... | collective-permute-start | bytes 663560 | tf_op jit(solution)/shard_map/ppermute | solution.py:44
  34.8 1.3 collective-permute-start.7
  36.7 1.4 constant_dynamic-slice_fusion.3
  38.7 3.0 collective-permute-done.5.small_oth.refs_8_
  41.7 2.8 collective-permute-done.6.x3
  45.2 5.0 %project.1 = (bf16[192,1024]{1,0:T(8,128)(2,1)}, bf16[384,1024]{1,0:T(8,128)(2,1)}) custom-call(s32[3]{0:T(128)} %get-tuple-element.202.scal.refs_0_.place, bf16[256,768]{1,0:T(8,128)(2,1)} %bitcast.72, bf16[256,768]{1,0:T(8,128)(2,1)} %copy-done.13, bf16[256,768]{1,0:T(8,128)(2,1)} %copy-done.12, bf16[256,768]{1,0:T(8,128)(2,1)} %copy-done.14, ...), custom_call_target="tpu_custom_call" | custom-call | flops 1 | bytes 1 | tf_op jit(solution)/shard_map/project/pallas_call | solution.py:543
  50.2 1.3 collective-permute-start.9
  51.5 3.6 %collective-permute-start.12 = (bf16[192,768]{1,0:T(8,128)(2,1)}, bf16[192,768]{1,0:T(8,128)(2,1)S(1)}, u32[]{:S(2)}, u32[]{:S(2)}) collective-permute-start(bf16[192,768]{1,0:T(8,128)(2,1)} %collective-permute-done.refs_10_), channel_id=1, source_target_pairs={{0,2},{2,0},{4,6},{6,4},{8,10},{10,8},{12,14},{14,12},{16,18},{18,... | collective-permute-start | bytes 884744 | tf_op jit(solution)/shard_map/ppermute | solution.py:44
  56.9 11.8 %collective-permute-done.11.refs_18_ = bf16[192,768]{1,0:T(8,128)(2,1)S(1)} collective-permute-done((bf16[192,768]{1,0:T(8,128)(2,1)S(1)}, bf16[192,768]{1,0:T(8,128)(2,1)S(1)}, u32[]{:S(2)}, u32[]{:S(2)}) %collective-permute-start.11) | collective-permute-done | bytes 294944 | tf_op jit(solution)/shard_map/ppermute | solution.py:44
  68.8 4.3 %collective-permute-start.14 = (bf16[384,1024]{1,0:T(8,128)(2,1)S(1)}, bf16[384,1024]{1,0:T(8,128)(2,1)S(1)}, u32[]{:S(2)}, u32[]{:S(2)}) collective-permute-start(bf16[384,1024]{1,0:T(8,128)(2,1)S(1)} %collective-permute-done.9.rest_2_.rest_6_), channel_id=1, source_target_pairs={{0,2},{2,0},{4,6},{6,4},{8,10},{10,8},{12,14},{14,12},{16,18},{18,... | collective-permute-start | bytes 2359304 | tf_op jit(solution)/shard_map/ppermute | solution.py:44
  73.1 1.9 collective-permute-done.14.rest_3_.rest_7_
  77.0 14.7 %group_fwd.1 = (f32[192,1024]{1,0:T(8,128)}, f32[3,1024]{1,0:T(4,128)}, bf16[192,256]{1,0:T(8,128)(2,1)}, bf16[192,256]{1,0:T(8,128)(2,1)}, bf16[192,256]{1,0:T(8,128)(2,1)}, /*index=5*/bf16[192,256]{1,0:T(8,128)(2,1)}) custom-call(s32[18]{0:T(128)} %concatenate.13.scal, s32[1,1024]{1,0:T(1,128)} %bitcast.95, s32[1,1024]{1,0:T(1,128)} %bitcast.93, ...), custom_call_target="tpu_custom_call" | custom-call | flops 1 | bytes 1 | tf_op jit(solution)/shard_map/group_fwd/pallas_call | solution.py:705
  91.6 4.4 %collective-permute-done.15.refs_19_ = bf16[576,768]{1,0:T(8,128)(2,1)S(1)} collective-permute-done((bf16[576,768]{1,0:T(8,128)(2,1)S(1)}, bf16[576,768]{1,0:T(8,128)(2,1)S(1)}, u32[]{:S(2)}, u32[]{:S(2)}) %collective-permute-start.15) | collective-permute-done | bytes 884768 | tf_op jit(solution)/shard_map/ppermute | solution.py:44
  97.5 1.5 collective-permute-start.19
  99.0 1.9 collective-permute-start.20
  100.9 2.1 collective-permute-done.18.refs_2_
  103.0 3.9 %collective-permute-done.19.refs_3_ = bf16[192,256]{1,0:T(8,128)(2,1)S(1)} collective-permute-done((bf16[192,256]{1,0:T(8,128)(2,1)}, bf16[192,256]{1,0:T(8,128)(2,1)S(1)}, u32[]{:S(2)}, u32[]{:S(2)}) %collective-permute-start.19) | collective-permute-done | bytes 98336 | tf_op jit(solution)/shard_map/ppermute | solution.py:44
  107.9 22.5 %middle.1 = (bf16[256,768]{1,0:T(8,128)(2,1)}, f32[256,768]{1,0:T(8,128)}, bf16[192,256]{1,0:T(8,128)(2,1)}, bf16[192,256]{1,0:T(8,128)(2,1)}, bf16[192,256]{1,0...) custom-call(s32[3]{0:T(128)} %get-tuple-element.202.scal.refs_0_.pla, ...), custom_call_target="tpu_custom_call" | custom-call | flops 1 | bytes 1 | tf_op jit(solution)/shard_map/middle/pallas_call | solution.py:1044
  130.4 2.0 collective-permute-start.26
  132.5 1.6 collective-permute-start.23
  134.2 2.1 collective-permute-start.25
  137.5 3.2 fusion
  141.4 2.7 add_convert_fusion
  146.5 1.6 collective-permute-start.34
  148.1 18.4 %group_bwd.1 = (bf16[192,1024]{1,0:T(8,128)(2,1)}, bf16[384,1024]{1,0:T(8,128)(2,1)}, bf16[384,1024]{1,0:T(8,128)(2,1)}, bf16[384,1024]{1,0:T(8,128)(2,1)}, bf16[384,1024]{1,0:T(8,128)(2,1)}) custom-call(s32[18]{0:T(128)} %concatenate.13.scal, s32[1,1024]{1,0:T(1,128)} %bitcast.96, s32[1,1024]{1,0:T(1,128)} %bitcast.94, ...), custom_call_target="tpu_custom_call" | custom-call | flops 1 | bytes 1 | tf_op jit(solution)/shard_map/group_bwd/pallas_call | solution.py:799
  166.5 8.7 %collective-permute-done.28 = bf16[896,768]{1,0:T(8,128)(2,1)} collective-permute-done((bf16[896,768]{1,0:T(8,128)(2,1)}, bf16[896,768]{1,0:T(8,128)(2,1)}, u32[]{:S(2)}, u32[]{:S(2)}) %collective-permute-start.28) | collective-permute-done | bytes 1376288 | tf_op jit(solution)/shard_map/ppermute | solution.py:44
  175.9 1.7 fusion.4
  177.6 2.3 collective-permute-start.32
  180.1 1.7 fusion.5
  183.6 14.9 %collective-permute-done.31 = bf16[448,768]{1,0:T(8,128)(2,1)S(1)} collective-permute-done((bf16[448,768]{1,0:T(8,128)(2,1)S(1)}, bf16[448,768]{1,0:T(8,128)(2,1)S(1)}, u32[]{:S(2)}, u32[]{:S(2)}) %collective-permute-start.31) | collective-permute-done | bytes 688160 | tf_op jit(solution)/shard_map/ppermute | solution.py:44
  199.5 1.9 fusion.3
  201.4 1.9 fusion.1
  207.4 1.6 collective-permute-start.36
  209.0 2.1 collective-permute-start.38
  211.1 3.4 turn.1.xt
  214.4 9.9 %collective-permute-done.37.refs_12_ = bf16[192,256]{1,0:T(8,128)(2,1)S(1)} collective-permute-done((bf16[192,256]{1,0:T(8,128)(2,1)S(1)}, bf16[192,256]{1,0:T(8,128)(2,1)S(1)}, u32[]{:S(2)}, u32[]{:S(2)}) %collective-permute-start.37) | collective-permute-done | bytes 98336 | tf_op jit(solution)/shard_map/ppermute | solution.py:44
  224.4 1.3 add_convert_fusion.2.dkv_ref
  225.7 4.7 %qkv_grad.1 = (bf16[2,208,576]{2,1,0:T(8,128)(2,1)}, bf16[2,208,576]{2,1,0:T(8,128)(2,1)}) custom-call(s32[3]{0:T(128)} %get-tuple-element.202.scal.refs_0_.place, bf16[768,1024]{1,0:T(8,128)(2,1)} %turn.1.xt, bf16[192,1024]{1,0:T(8,128)(2,1)} %get-tuple-element.304.dq_ref, bf16[384,1024]{1,0:T(8,128)(2,1)} %add_convert_fusion.2.dkv_ref), custom_call_target="tpu_custom_call" | custom-call | tf_op jit(solution)/shard_map/qkv_grad/pallas_call | solution.py:1144
  231.5 1.8 collective-permute-done.39
  234.2 8.0 %reduce-scatter.2.cloned.1.call-done = bf16[224,768]{1,0:T(8,128)(2,1)} async-done(((bf16[896,768]{1,0:T(8,128)(2,1)}), bf16[224,768]{1,0:T(8,128)(2,1)}) %reduce-scatter.2.cloned.1.call-update) | async-done | bytes 344080 | tf_op jit(solution)/shard_map/reduce_scatter | solution.py:1521
  242.2 1.7 fusion.18
  245.0 1.9 collective-permute-start.42
  246.8 3.8 %collective-permute-done.40 = bf16[208,576]{1,0:T(8,128)(2,1)S(1)} collective-permute-done((bf16[208,576]{1,0:T(8,128)(2,1)S(1)}, bf16[208,576]{1,0:T(8,128)(2,1)S(1)}, u32[]{:S(2)}, u32[]{:S(2)}) %collective-permute-start.40) | collective-permute-done | bytes 239648 | tf_op jit(solution)/shard_map/ppermute | solution.py:44
  251.1 3.2 collective-permute-start.44
  255.0 3.0 collective-permute-start.43
  258.1 12.2 %collective-permute-done.44 = bf16[2,112,768]{2,1,0:T(8,128)(2,1)S(1)} collective-permute-done((bf16[2,112,768]{2,1,0:T(8,128)(2,1)S(1)}, bf16[2,112,768]{2,1,0:T(8,128)(2,1)S(1)}, u32[]{:S(2)}, u32[]{:S(2)}) %collective-permute-start.44) | collective-permute-done | bytes 344096 | tf_op jit(solution)/shard_map/ppermute | solution.py:44
  270.7 3.0 collective-permute-start.46
  273.7 7.7 %collective-permute-done.45 = bf16[2,104,576]{2,1,0:T(8,128)(2,1)S(1)} collective-permute-done((bf16[2,104,576]{2,1,0:T(8,128)(2,1)S(1)}, bf16[2,104,576]{2,1,0:T(8,128)(2,1)S(1)}, u32[]{:S(2)}, u32[]{:S(2)}) %collective-permute-start.45) | collective-permute-done | bytes 239648 | tf_op jit(solution)/shard_map/ppermute | solution.py:44
  281.6 3.8 %collective-permute-start.47 = (bf16[4,104,576]{2,1,0:T(8,128)(2,1)S(1)}, bf16[4,104,576]{2,1,0:T(8,128)(2,1)}, u32[]{:S(2)}, u32[]{:S(2)}) collective-permute-start(bf16[4,104,576]{2,1,0:T(8,128)(2,1)S(1)} %bitcast.79), channel_id=1, source_target_pairs={{0,4},{2,6},{4,0},{6,2},{8,12},{10,14},{12,8},{14,10},{16,20},{18,... | collective-permute-start | bytes 1437704 | tf_op jit(solution)/shard_map/ppermute | solution.py:44
  286.2 2.2 collective-permute-start.48
  288.5 2.1 collective-permute-start.50
  290.5 3.8 %collective-permute-done.48.refs_15_ = bf16[384,256]{1,0:T(8,128)(2,1)} collective-permute-done((bf16[384,256]{1,0:T(8,128)(2,1)S(1)}, bf16[384,256]{1,0:T(8,128)(2,1)}, u32[]{:S(2)}, u32[]{:S(2)}) %collective-permute-start.48) | collective-permute-done | bytes 196640 | tf_op jit(solution)/shard_map/ppermute | solution.py:44
  294.4 6.4 %collective-permute-start.53 = (bf16[2,2,112,768]{3,2,1,0:T(8,128)(2,1)S(1)}, bf16[2,2,112,768]{3,2,1,0:T(8,128)(2,1)S(1)}, u32[]{:S(2)}, u32[]{:S(2)}) collective-permute-start(bf16[2,2,112,768]{3,2,1,0:T(8,128)(2,1)S(1)} %pad_maximum_fusion.1), channel_id=1, source_target_pairs={{0,2},{2,0},{4,6},{6,4},{8,10},{10,8},{12,14},{14,12},{16,18},{18,... | collective-permute-start | bytes 2064392 | tf_op jit(solution)/shard_map/ppermute | solution.py:44
  300.7 6.6 %collective-permute-done.49.refs_16_ = bf16[384,256]{1,0:T(8,128)(2,1)S(1)} collective-permute-done((bf16[384,256]{1,0:T(8,128)(2,1)S(1)}, bf16[384,256]{1,0:T(8,128)(2,1)S(1)}, u32[]{:S(2)}, u32[]{:S(2)}) %collective-permute-start.49) | collective-permute-done | bytes 196640 | tf_op jit(solution)/shard_map/ppermute | solution.py:44
  308.0 2.2 collective-permute-start.54
  310.7 2.8 collective-permute-done.51.refs_7_
  314.7 10.4 %ending.1 = (f32[1536,768]{1,0:T(8,128)}, f32[384,3072]{1,0:T(8,128)}, f32[384,768]{1,0:T(8,128)}, f32[8,768]{1,0:T(8,128)}, f32[384,768]{1,0:T(8,128)}, /*index...) custom-call(s32[3]{0:T(128)} %get-tuple-element.202.scal.refs_0_.place, ...), custom_call_target="tpu_custom_call" | custom-call | flops 1 | bytes 1 | tf_op jit(solution)/shard_map/ending/pallas_call | solution.py:1301
  326.4 1.3 slice_reduce_fusion.2
  327.8 1.6 dynamic-slice_reduce_fusion
  (228 shorter events, 43.6 us)
Async XLA Ops:
  7.2 235.0 %reduce-scatter.2.cloned.1.call-start = ((), (), s32[]{:S(2)}) async-start(), calls=%async_computation.1 | async-start | bytes 1720320 | tf_op jit(solution)/shard_map/reduce_scatter | solution.py:1521
  7.2 24.1 %collective-permute-start.3 = (bf16[256,768]{1,0:T(8,128)(2,1)}, bf16[256,768]{1,0:T(8,128)(2,1)S(1)}, u32[]{:S(2)}, u32[]{:S(2)}) collective-permute-start(bf16[256,768]{1,0:T(8,128)(2,1)} %bitcast.70), channel_id=1, source_target_pairs={{0,16},{2,18},{4,20},{6,22},{8,24},{10,26},{12,28},{14,30},{16,0},... | collective-permute-start | bytes 1179656 | tf_op jit(solution)/shard_map/ppermute | solution.py:44
  10.4 20.9 %collective-permute-start.4 = (bf16[256,768]{1,0:T(8,128)(2,1)}, bf16[256,768]{1,0:T(8,128)(2,1)S(1)}, u32[]{:S(2)}, u32[]{:S(2)}) collective-permute-start(bf16[256,768]{1,0:T(8,128)(2,1)} %bitcast.71), channel_id=1, source_target_pairs={{0,8},{2,10},{4,12},{6,14},{8,0},{10,2},{12,4},{14,6},{16,24},{18,... | collective-permute-start | bytes 1179656 | tf_op jit(solution)/shard_map/ppermute | solution.py:44
  12.8 20.0 %copy-start.1 = (bf16[384,3072]{1,0:T(8,128)(2,1)S(1)}, bf16[384,3072]{1,0:T(8,128)(2,1)}, u32[]{:S(2)}) copy-start(bf16[384,3072]{1,0:T(8,128)(2,1)} %refs_12_.1) | copy-start | bytes 7077892
  18.4 6.5 %collective-permute-start.1 = (bf16[192,576]{1,0:T(8,128)(2,1)}, bf16[192,576]{1,0:T(8,128)(2,1)}, u32[]{:S(2)}, u32[]{:S(2)}) collective-permute-start(bf16[192,576]{1,0:T(8,128)(2,1)} %constant_dynamic-slice_fusion.5), channel_id=1, source_target_pairs={{0,1},{1,0},{2,3},{3,2},{4,5},{5,4},{6,7},{7,6},{8,9},{9,8},{10,11... | collective-permute-start | bytes 663560 | tf_op jit(solution)/shard_map/ppermute | solution.py:44
  20.7 10.6 %collective-permute-start = (bf16[192,768]{1,0:T(8,128)(2,1)S(1)}, bf16[192,768]{1,0:T(8,128)(2,1)}, u32[]{:S(2)}, u32[]{:S(2)}) collective-permute-start(bf16[192,768]{1,0:T(8,128)(2,1)S(1)} %constant_dynamic-slice_fusion.9), channel_id=1, source_target_pairs={{0,1},{1,0},{2,3},{3,2},{4,5},{5,4},{6,7},{7,6},{8,9},{9,8},{10,11... | collective-permute-start | bytes 884744 | tf_op jit(solution)/shard_map/ppermute | solution.py:44
  25.0 7.8 %collective-permute-start.2 = (bf16[192,576]{1,0:T(8,128)(2,1)}, bf16[192,576]{1,0:T(8,128)(2,1)}, u32[]{:S(2)}, u32[]{:S(2)}) collective-permute-start(bf16[192,576]{1,0:T(8,128)(2,1)} %collective-permute-done.1.mine), channel_id=1, source_target_pairs={{0,2},{2,0},{4,6},{6,4},{8,10},{10,8},{12,14},{14,12},{16,18},{18,... | collective-permute-start | bytes 663560 | tf_op jit(solution)/shard_map/ppermute | solution.py:44
  34.8 6.9 %collective-permute-start.7 = (bf16[48,3072]{1,0:T(8,128)(2,1)}, bf16[48,3072]{1,0:T(8,128)(2,1)S(1)}, u32[]{:S(2)}, u32[]{:S(2)}) collective-permute-start(bf16[48,3072]{1,0:T(8,128)(2,1)} %constant_dynamic-slice_fusion.1), channel_id=1, source_target_pairs={{0,1},{1,0},{2,3},{3,2},{4,5},{5,4},{6,7},{7,6},{8,9},{9,8},{10,11... | collective-permute-start | bytes 884744 | tf_op jit(solution)/shard_map/ppermute | solution.py:44
  36.1 8.4 %collective-permute-start.6 = (bf16[256,768]{1,0:T(8,128)(2,1)}, bf16[256,768]{1,0:T(8,128)(2,1)S(1)}, u32[]{:S(2)}, u32[]{:S(2)}) collective-permute-start(bf16[256,768]{1,0:T(8,128)(2,1)} %copy-done.12), channel_id=1, source_target_pairs={{0,8},{2,10},{4,12},{6,14},{8,0},{10,2},{12,4},{14,6},{16,24},{18,... | collective-permute-start | bytes 1179656 | tf_op jit(solution)/shard_map/ppermute | solution.py:44
  36.3 5.4 %collective-permute-start.5 = (bf16[12,384]{1,0:T(8,128)(2,1)S(1)}, bf16[12,384]{1,0:T(8,128)(2,1)S(1)}, u32[]{:S(2)}, u32[]{:S(2)}) collective-permute-start(bf16[12,384]{1,0:T(8,128)(2,1)S(1)} %copy-done.40), channel_id=1, source_target_pairs={{0,1},{1,0},{2,3},{3,2},{4,5},{5,4},{6,7},{7,6},{8,9},{9,8},{10,11... | collective-permute-start | bytes 27656 | tf_op jit(solution)/shard_map/ppermute | solution.py:44
  44.6 24.2 %collective-permute-start.10 = (bf16[144,3072]{1,0:T(8,128)(2,1)S(1)}, bf16[144,3072]{1,0:T(8,128)(2,1)S(1)}, u32[]{:S(2)}, u32[]{:S(2)}) collective-permute-start(bf16[144,3072]{1,0:T(8,128)(2,1)S(1)} %slice.86), channel_id=1, source_target_pairs={{0,1},{1,0},{2,3},{3,2},{4,5},{5,4},{6,7},{7,6},{8,9},{9,8},{10,11... | collective-permute-start | bytes 2654216 | tf_op jit(solution)/shard_map/ppermute | solution.py:44
  50.2 25.9 %copy-start.15 = (bf16[384,768]{1,0:T(8,128)(2,1)S(1)}, bf16[384,768]{1,0:T(8,128)(2,1)}, u32[]{:S(2)}) copy-start(bf16[384,768]{1,0:T(8,128)(2,1)} %param.19) | copy-start | bytes 1769476
  50.2 18.5 %collective-permute-start.9 = (bf16[384,1024]{1,0:T(8,128)(2,1)}, bf16[384,1024]{1,0:T(8,128)(2,1)S(1)}, u32[]{:S(2)}, u32[]{:S(2)}) collective-permute-start(bf16[384,1024]{1,0:T(8,128)(2,1)} %get-tuple-element.220.rest_0_.rest_4_), channel_id=1, source_target_pairs={{0,4},{2,6},{4,0},{6,2},{8,12},{10,14},{12,8},{14,10},{16,20},{18,... | collective-permute-start | bytes 2359304 | tf_op jit(solution)/shard_map/ppermute | solution.py:44
  51.5 5.2 %collective-permute-start.12 = (bf16[192,768]{1,0:T(8,128)(2,1)}, bf16[192,768]{1,0:T(8,128)(2,1)S(1)}, u32[]{:S(2)}, u32[]{:S(2)}) collective-permute-start(bf16[192,768]{1,0:T(8,128)(2,1)} %collective-permute-done.refs_10_), channel_id=1, source_target_pairs={{0,2},{2,0},{4,6},{6,4},{8,10},{10,8},{12,14},{14,12},{16,18},{18,... | collective-permute-start | bytes 884744 | tf_op jit(solution)/shard_map/ppermute | solution.py:44
  55.1 21.0 %copy-start.16 = (bf16[384,768]{1,0:T(8,128)(2,1)S(1)}, bf16[384,768]{1,0:T(8,128)(2,1)}, u32[]{:S(2)}) copy-start(bf16[384,768]{1,0:T(8,128)(2,1)} %param.21) | copy-start | bytes 1769476
  55.1 13.6 %collective-permute-start.11 = (bf16[192,768]{1,0:T(8,128)(2,1)S(1)}, bf16[192,768]{1,0:T(8,128)(2,1)S(1)}, u32[]{:S(2)}, u32[]{:S(2)}) collective-permute-start(bf16[192,768]{1,0:T(8,128)(2,1)S(1)} %slice.87), channel_id=1, source_target_pairs={{0,1},{1,0},{2,3},{3,2},{4,5},{5,4},{6,7},{7,6},{8,9},{9,8},{10,11... | collective-permute-start | bytes 884744 | tf_op jit(solution)/shard_map/ppermute | solution.py:44
  56.4 12.3 %collective-permute-start.13 = (bf16[48,3072]{1,0:T(8,128)(2,1)S(1)}, bf16[48,3072]{1,0:T(8,128)(2,1)S(1)}, u32[]{:S(2)}, u32[]{:S(2)}) collective-permute-start(bf16[48,3072]{1,0:T(8,128)(2,1)S(1)} %copy-done.33), channel_id=1, source_target_pairs={{0,2},{2,0},{4,6},{6,4},{8,10},{10,8},{12,14},{14,12},{16,18},{18,... | collective-permute-start | bytes 884744 | tf_op jit(solution)/shard_map/ppermute | solution.py:44
  56.7 16.4 %collective-permute-start.8 = (bf16[384,1024]{1,0:T(8,128)(2,1)}, bf16[384,1024]{1,0:T(8,128)(2,1)S(1)}, u32[]{:S(2)}, u32[]{:S(2)}) collective-permute-start(bf16[384,1024]{1,0:T(8,128)(2,1)} %get-tuple-element.220.rest_0_.rest_4_), channel_id=1, source_target_pairs={{0,2},{2,0},{4,6},{6,4},{8,10},{10,8},{12,14},{14,12},{16,18},{18,... | collective-permute-start | bytes 2359304 | tf_op jit(solution)/shard_map/ppermute | solution.py:44
  68.8 6.3 %collective-permute-start.14 = (bf16[384,1024]{1,0:T(8,128)(2,1)S(1)}, bf16[384,1024]{1,0:T(8,128)(2,1)S(1)}, u32[]{:S(2)}, u32[]{:S(2)}) collective-permute-start(bf16[384,1024]{1,0:T(8,128)(2,1)S(1)} %collective-permute-done.9.rest_2_.rest_6_), channel_id=1, source_target_pairs={{0,2},{2,0},{4,6},{6,4},{8,10},{10,8},{12,14},{14,12},{16,18},{18,... | collective-permute-start | bytes 2359304 | tf_op jit(solution)/shard_map/ppermute | solution.py:44
  75.1 20.9 %collective-permute-start.15 = (bf16[576,768]{1,0:T(8,128)(2,1)S(1)}, bf16[576,768]{1,0:T(8,128)(2,1)S(1)}, u32[]{:S(2)}, u32[]{:S(2)}) collective-permute-start(bf16[576,768]{1,0:T(8,128)(2,1)S(1)} %slice.88), channel_id=1, source_target_pairs={{0,1},{1,0},{2,3},{3,2},{4,5},{5,4},{6,7},{7,6},{8,9},{9,8},{10,11... | collective-permute-start | bytes 2654216 | tf_op jit(solution)/shard_map/ppermute | solution.py:44
  75.4 20.6 %collective-permute-start.16 = (bf16[144,3072]{1,0:T(8,128)(2,1)S(1)}, bf16[144,3072]{1,0:T(8,128)(2,1)S(1)}, u32[]{:S(2)}, u32[]{:S(2)}) collective-permute-start(bf16[144,3072]{1,0:T(8,128)(2,1)S(1)} %collective-permute-done.10.refs_14_), channel_id=1, source_target_pairs={{0,2},{2,0},{4,6},{6,4},{8,10},{10,8},{12,14},{14,12},{16,18},{18,... | collective-permute-start | bytes 2654216 | tf_op jit(solution)/shard_map/ppermute | solution.py:44
  76.5 15.2 %collective-permute-start.17 = (bf16[192,768]{1,0:T(8,128)(2,1)S(1)}, bf16[192,768]{1,0:T(8,128)(2,1)S(1)}, u32[]{:S(2)}, u32[]{:S(2)}) collective-permute-start(bf16[192,768]{1,0:T(8,128)(2,1)S(1)} %collective-permute-done.11.refs_18_), channel_id=1, source_target_pairs={{0,2},{2,0},{4,6},{6,4},{8,10},{10,8},{12,14},{14,12},{16,18},{18,... | collective-permute-start | bytes 884744 | tf_op jit(solution)/shard_map/ppermute | solution.py:44
  96.1 10.9 %collective-permute-start.21 = (bf16[576,768]{1,0:T(8,128)(2,1)S(1)}, bf16[576,768]{1,0:T(8,128)(2,1)S(1)}, u32[]{:S(2)}, u32[]{:S(2)}) collective-permute-start(bf16[576,768]{1,0:T(8,128)(2,1)S(1)} %collective-permute-done.15.refs_19_), channel_id=1, source_target_pairs={{0,2},{2,0},{4,6},{6,4},{8,10},{10,8},{12,14},{14,12},{16,18},{18,... | collective-permute-start | bytes 2654216 | tf_op jit(solution)/shard_map/ppermute | solution.py:44
  97.3 5.7 %collective-permute-start.18 = (bf16[192,256]{1,0:T(8,128)(2,1)}, bf16[192,256]{1,0:T(8,128)(2,1)S(1)}, u32[]{:S(2)}, u32[]{:S(2)}) collective-permute-start(bf16[192,256]{1,0:T(8,128)(2,1)} %get-tuple-element.236), channel_id=1, source_target_pairs={{0,8},{2,10},{4,12},{6,14},{8,0},{10,2},{12,4},{14,6},{16,24},{18,... | collective-permute-start | bytes 294920 | tf_op jit(solution)/shard_map/ppermute | solution.py:44
  97.5 9.4 %collective-permute-start.19 = (bf16[192,256]{1,0:T(8,128)(2,1)}, bf16[192,256]{1,0:T(8,128)(2,1)S(1)}, u32[]{:S(2)}, u32[]{:S(2)}) collective-permute-start(bf16[192,256]{1,0:T(8,128)(2,1)} %get-tuple-element.237), channel_id=1, source_target_pairs={{0,16},{2,18},{4,20},{6,22},{8,24},{10,26},{12,28},{14,30},{16,0},... | collective-permute-start | bytes 294920 | tf_op jit(solution)/shard_map/ppermute | solution.py:44
  99.0 7.9 %collective-permute-start.20 = (bf16[192,256]{1,0:T(8,128)(2,1)}, bf16[192,256]{1,0:T(8,128)(2,1)S(1)}, u32[]{:S(2)}, u32[]{:S(2)}) collective-permute-start(bf16[192,256]{1,0:T(8,128)(2,1)} %get-tuple-element.238), channel_id=1, source_target_pairs={{0,24},{2,26},{4,28},{6,30},{8,16},{10,18},{12,20},{14,22},{16,8},... | collective-permute-start | bytes 294920 | tf_op jit(solution)/shard_map/ppermute | solution.py:44
  107.0 23.5 %collective-permute-start.22 = (bf16[192,2304]{1,0:T(8,128)(2,1)S(1)}, bf16[192,2304]{1,0:T(8,128)(2,1)S(1)}, u32[]{:S(2)}, u32[]{:S(2)}) collective-permute-start(bf16[192,2304]{1,0:T(8,128)(2,1)S(1)} %constant_dynamic-slice_fusion.2), channel_id=1, source_target_pairs={{0,1},{1,0},{2,3},{3,2},{4,5},{5,4},{6,7},{7,6},{8,9},{9,8},{10,11... | collective-permute-start | bytes 2654216 | tf_op jit(solution)/shard_map/ppermute | solution.py:44
  130.4 7.1 %collective-permute-start.26 = (bf16[2,896,768]{2,1,0:T(8,128)(2,1)}, bf16[2,896,768]{2,1,0:T(8,128)(2,1)}, u32[]{:S(2)}, u32[]{:S(2)}) collective-permute-start(bf16[2,896,768]{2,1,0:T(8,128)(2,1)} %get-tuple-element.270), channel_id=1, source_target_pairs={{0,2},{2,0},{4,6},{6,4},{8,10},{10,8},{12,14},{14,12},{16,18},{18,... | collective-permute-start | bytes 8257544 | tf_op jit(solution)/shard_map/ppermute | solution.py:44
  132.4 9.0 %collective-permute-start.27 = (bf16[2,896,768]{2,1,0:T(8,128)(2,1)}, bf16[2,896,768]{2,1,0:T(8,128)(2,1)}, u32[]{:S(2)}, u32[]{:S(2)}) collective-permute-start(bf16[2,896,768]{2,1,0:T(8,128)(2,1)} %get-tuple-element.273), channel_id=1, source_target_pairs={{0,2},{2,0},{4,6},{6,4},{8,10},{10,8},{12,14},{14,12},{16,18},{18,... | collective-permute-start | bytes 8257544 | tf_op jit(solution)/shard_map/ppermute | solution.py:44
  132.5 11.7 %collective-permute-start.23 = (bf16[192,256]{1,0:T(8,128)(2,1)}, bf16[192,256]{1,0:T(8,128)(2,1)S(1)}, u32[]{:S(2)}, u32[]{:S(2)}) collective-permute-start(bf16[192,256]{1,0:T(8,128)(2,1)} %get-tuple-element.266), channel_id=1, source_target_pairs={{0,8},{2,10},{4,12},{6,14},{8,0},{10,2},{12,4},{14,6},{16,24},{18,... | collective-permute-start | bytes 294920 | tf_op jit(solution)/shard_map/ppermute | solution.py:44
  134.1 10.1 %collective-permute-start.24 = (bf16[192,256]{1,0:T(8,128)(2,1)}, bf16[192,256]{1,0:T(8,128)(2,1)S(1)}, u32[]{:S(2)}, u32[]{:S(2)}) collective-permute-start(bf16[192,256]{1,0:T(8,128)(2,1)} %get-tuple-element.267), channel_id=1, source_target_pairs={{0,16},{2,18},{4,20},{6,22},{8,24},{10,26},{12,28},{14,30},{16,0},... | collective-permute-start | bytes 294920 | tf_op jit(solution)/shard_map/ppermute | solution.py:44
  134.2 10.0 %collective-permute-start.25 = (bf16[192,256]{1,0:T(8,128)(2,1)}, bf16[192,256]{1,0:T(8,128)(2,1)S(1)}, u32[]{:S(2)}, u32[]{:S(2)}) collective-permute-start(bf16[192,256]{1,0:T(8,128)(2,1)} %get-tuple-element.268), channel_id=1, source_target_pairs={{0,24},{2,26},{4,28},{6,30},{8,16},{10,18},{12,20},{14,22},{16,8},... | collective-permute-start | bytes 294920 | tf_op jit(solution)/shard_map/ppermute | solution.py:44
  144.2 31.0 %collective-permute-start.28 = (bf16[896,768]{1,0:T(8,128)(2,1)}, bf16[896,768]{1,0:T(8,128)(2,1)}, u32[]{:S(2)}, u32[]{:S(2)}) collective-permute-start(bf16[896,768]{1,0:T(8,128)(2,1)} %fusion), channel_id=1, source_target_pairs={{0,1},{1,0},{2,3},{3,2},{4,5},{5,4},{6,7},{7,6},{8,9},{9,8},{10,11... | collective-permute-start | bytes 4128776 | tf_op jit(solution)/shard_map/ppermute | solution.py:44
  145.3 30.6 %collective-permute-start.29 = (bf16[2,448,768]{2,1,0:T(8,128)(2,1)}, bf16[2,448,768]{2,1,0:T(8,128)(2,1)}, u32[]{:S(2)}, u32[]{:S(2)}) collective-permute-start(bf16[2,448,768]{2,1,0:T(8,128)(2,1)} %add_convert_fusion), channel_id=1, source_target_pairs={{0,4},{2,6},{4,0},{6,2},{8,12},{10,14},{12,8},{14,10},{16,20},{18,... | collective-permute-start | bytes 4128776 | tf_op jit(solution)/shard_map/ppermute | solution.py:44
  146.5 29.4 %copy-start.8 = (bf16[2,896,768]{2,1,0:T(8,128)(2,1)S(1)}, bf16[2,896,768]{2,1,0:T(8,128)(2,1)}, u32[]{:S(2)}) copy-start(bf16[2,896,768]{2,1,0:T(8,128)(2,1)} %get-tuple-element.269) | copy-start | bytes 8257540
  146.5 37.1 %collective-permute-start.34 = (bf16[192,2304]{1,0:T(8,128)(2,1)}, bf16[192,2304]{1,0:T(8,128)(2,1)S(1)}, u32[]{:S(2)}, u32[]{:S(2)}) collective-permute-start(bf16[192,2304]{1,0:T(8,128)(2,1)} %copy-done.18), channel_id=1, source_target_pairs={{0,2},{2,0},{4,6},{6,4},{8,10},{10,8},{12,14},{14,12},{16,18},{18,... | collective-permute-start | bytes 2654216 | tf_op jit(solution)/shard_map/ppermute | solution.py:44
  177.6 21.0 %collective-permute-start.32 = (bf16[384,1024]{1,0:T(8,128)(2,1)S(1)}, bf16[384,1024]{1,0:T(8,128)(2,1)S(1)}, u32[]{:S(2)}, u32[]{:S(2)}) collective-permute-start(bf16[384,1024]{1,0:T(8,128)(2,1)S(1)} %copy-done.55), channel_id=1, source_target_pairs={{0,2},{2,0},{4,6},{6,4},{8,10},{10,8},{12,14},{14,12},{16,18},{18,... | collective-permute-start | bytes 2359304 | tf_op jit(solution)/shard_map/ppermute | solution.py:44
  180.0 18.7 %collective-permute-start.33 = (bf16[384,1024]{1,0:T(8,128)(2,1)S(1)}, bf16[384,1024]{1,0:T(8,128)(2,1)S(1)}, u32[]{:S(2)}, u32[]{:S(2)}) collective-permute-start(bf16[384,1024]{1,0:T(8,128)(2,1)S(1)} %copy-done.54), channel_id=1, source_target_pairs={{0,2},{2,0},{4,6},{6,4},{8,10},{10,8},{12,14},{14,12},{16,18},{18,... | collective-permute-start | bytes 2359304 | tf_op jit(solution)/shard_map/ppermute | solution.py:44
  181.8 16.6 %collective-permute-start.31 = (bf16[448,768]{1,0:T(8,128)(2,1)S(1)}, bf16[448,768]{1,0:T(8,128)(2,1)S(1)}, u32[]{:S(2)}, u32[]{:S(2)}) collective-permute-start(bf16[448,768]{1,0:T(8,128)(2,1)S(1)} %fusion.5), channel_id=1, source_target_pairs={{0,1},{1,0},{2,3},{3,2},{4,5},{5,4},{6,7},{7,6},{8,9},{9,8},{10,11... | collective-permute-start | bytes 2064392 | tf_op jit(solution)/shard_map/ppermute | solution.py:44
  182.4 16.3 %collective-permute-start.30 = (bf16[448,768]{1,0:T(8,128)(2,1)S(1)}, bf16[448,768]{1,0:T(8,128)(2,1)S(1)}, u32[]{:S(2)}, u32[]{:S(2)}) collective-permute-start(bf16[448,768]{1,0:T(8,128)(2,1)S(1)} %fusion.4), channel_id=1, source_target_pairs={{0,4},{2,6},{4,0},{6,2},{8,12},{10,14},{12,8},{14,10},{16,20},{18,... | collective-permute-start | bytes 2064392 | tf_op jit(solution)/shard_map/ppermute | solution.py:44
  204.5 109.3 %all-gather.3.cloned.1.call-start = ((), (), s32[]{:S(2)}) async-start(), calls=%async_computation.2 | async-start | bytes 2924544 | tf_op jit(solution)/shard_map/all_gather | solution.py:1540
  205.5 18.9 %collective-permute-start.35 = (bf16[384,1024]{1,0:T(8,128)(2,1)S(1)}, bf16[384,1024]{1,0:T(8,128)(2,1)S(1)}, u32[]{:S(2)}, u32[]{:S(2)}) collective-permute-start(bf16[384,1024]{1,0:T(8,128)(2,1)S(1)} %add_convert_fusion.3), channel_id=1, source_target_pairs={{0,4},{2,6},{4,0},{6,2},{8,12},{10,14},{12,8},{14,10},{16,20},{18,... | collective-permute-start | bytes 2359304 | tf_op jit(solution)/shard_map/ppermute | solution.py:44
  207.4 7.0 %collective-permute-start.36 = (bf16[192,256]{1,0:T(8,128)(2,1)S(1)}, bf16[192,256]{1,0:T(8,128)(2,1)S(1)}, u32[]{:S(2)}, u32[]{:S(2)}) collective-permute-start(bf16[192,256]{1,0:T(8,128)(2,1)S(1)} %get-tuple-element.306), channel_id=1, source_target_pairs={{0,8},{2,10},{4,12},{6,14},{8,0},{10,2},{12,4},{14,6},{16,24},{18,... | collective-permute-start | bytes 294920 | tf_op jit(solution)/shard_map/ppermute | solution.py:44
  209.0 15.4 %collective-permute-start.37 = (bf16[192,256]{1,0:T(8,128)(2,1)S(1)}, bf16[192,256]{1,0:T(8,128)(2,1)S(1)}, u32[]{:S(2)}, u32[]{:S(2)}) collective-permute-start(bf16[192,256]{1,0:T(8,128)(2,1)S(1)} %get-tuple-element.307), channel_id=1, source_target_pairs={{0,16},{2,18},{4,20},{6,22},{8,24},{10,26},{12,28},{14,30},{16,0},... | collective-permute-start | bytes 294920 | tf_op jit(solution)/shard_map/ppermute | solution.py:44
  209.0 15.3 %collective-permute-start.38 = (bf16[192,256]{1,0:T(8,128)(2,1)S(1)}, bf16[192,256]{1,0:T(8,128)(2,1)S(1)}, u32[]{:S(2)}, u32[]{:S(2)}) collective-permute-start(bf16[192,256]{1,0:T(8,128)(2,1)S(1)} %get-tuple-element.308), channel_id=1, source_target_pairs={{0,24},{2,26},{4,28},{6,30},{8,16},{10,18},{12,20},{14,22},{16,8},... | collective-permute-start | bytes 294920 | tf_op jit(solution)/shard_map/ppermute | solution.py:44
  230.3 20.3 %copy-start.31 = (bf16[2,208,576]{2,1,0:T(8,128)(2,1)S(1)}, bf16[2,208,576]{2,1,0:T(8,128)(2,1)}, u32[]{:S(2)}) copy-start(bf16[2,208,576]{2,1,0:T(8,128)(2,1)} %get-tuple-element.314) | copy-start | bytes 1437700
  230.3 2.9 collective-permute-start.39
  243.9 6.7 %collective-permute-start.40 = (bf16[208,576]{1,0:T(8,128)(2,1)S(1)}, bf16[208,576]{1,0:T(8,128)(2,1)S(1)}, u32[]{:S(2)}, u32[]{:S(2)}) collective-permute-start(bf16[208,576]{1,0:T(8,128)(2,1)S(1)} %fusion.7), channel_id=1, source_target_pairs={{0,1},{1,0},{2,3},{3,2},{4,5},{5,4},{6,7},{7,6},{8,9},{9,8},{10,11... | collective-permute-start | bytes 718856 | tf_op jit(solution)/shard_map/ppermute | solution.py:44
  245.0 6.1 %collective-permute-start.42 = (bf16[112,768]{1,0:T(8,128)(2,1)S(1)}, bf16[112,768]{1,0:T(8,128)(2,1)S(1)}, u32[]{:S(2)}, u32[]{:S(2)}) collective-permute-start(bf16[112,768]{1,0:T(8,128)(2,1)S(1)} %get-tuple-element.405), channel_id=1, source_target_pairs={{0,16},{2,18},{4,20},{6,22},{8,24},{10,26},{12,28},{14,30},{16,0},... | collective-permute-start | bytes 516104 | tf_op jit(solution)/shard_map/ppermute | solution.py:44
  250.7 4.2 %collective-permute-start.41 = (bf16[104,576]{1,0:T(8,128)(2,1)S(1)}, bf16[104,576]{1,0:T(8,128)(2,1)S(1)}, u32[]{:S(2)}, u32[]{:S(2)}) collective-permute-start(bf16[104,576]{1,0:T(8,128)(2,1)S(1)} %fusion.8), channel_id=1, source_target_pairs={{0,4},{2,6},{4,0},{6,2},{8,12},{10,14},{12,8},{14,10},{16,20},{18,... | collective-permute-start | bytes 359432 | tf_op jit(solution)/shard_map/ppermute | solution.py:44
  251.1 19.2 %collective-permute-start.44 = (bf16[2,112,768]{2,1,0:T(8,128)(2,1)S(1)}, bf16[2,112,768]{2,1,0:T(8,128)(2,1)S(1)}, u32[]{:S(2)}, u32[]{:S(2)}) collective-permute-start(bf16[2,112,768]{2,1,0:T(8,128)(2,1)S(1)} %pad_maximum_fusion.3), channel_id=1, source_target_pairs={{0,8},{2,10},{4,12},{6,14},{8,0},{10,2},{12,4},{14,6},{16,24},{18,... | collective-permute-start | bytes 1032200 | tf_op jit(solution)/shard_map/ppermute | solution.py:44
  255.0 15.3 %collective-permute-start.43 = (bf16[104,576]{1,0:T(8,128)(2,1)S(1)}, bf16[104,576]{1,0:T(8,128)(2,1)S(1)}, u32[]{:S(2)}, u32[]{:S(2)}) collective-permute-start(bf16[104,576]{1,0:T(8,128)(2,1)S(1)} %fusion.10), channel_id=1, source_target_pairs={{0,16},{2,18},{4,20},{6,22},{8,24},{10,26},{12,28},{14,30},{16,0},... | collective-permute-start | bytes 359432 | tf_op jit(solution)/shard_map/ppermute | solution.py:44
  270.3 24.0 %copy-start.9 = (bf16[2,2,112,768]{3,2,1,0:T(8,128)(2,1)}, bf16[2,2,112,768]{3,2,1,0:T(8,128)(2,1)S(1)}, u32[]{:S(2)}) copy-start(bf16[2,2,112,768]{3,2,1,0:T(8,128)(2,1)S(1)} %pad_maximum_fusion.1) | copy-start | bytes 2064388
  270.5 11.0 %collective-permute-start.45 = (bf16[2,104,576]{2,1,0:T(8,128)(2,1)S(1)}, bf16[2,104,576]{2,1,0:T(8,128)(2,1)S(1)}, u32[]{:S(2)}, u32[]{:S(2)}) collective-permute-start(bf16[2,104,576]{2,1,0:T(8,128)(2,1)S(1)} %maximum_select_fusion.1), channel_id=1, source_target_pairs={{0,8},{2,10},{4,12},{6,14},{8,0},{10,2},{12,4},{14,6},{16,24},{18,... | collective-permute-start | bytes 718856 | tf_op jit(solution)/shard_map/ppermute | solution.py:44
  270.7 36.6 %collective-permute-start.46 = (bf16[2,2,112,768]{3,2,1,0:T(8,128)(2,1)S(1)}, bf16[2,2,112,768]{3,2,1,0:T(8,128)(2,1)S(1)}, u32[]{:S(2)}, u32[]{:S(2)}) collective-permute-start(bf16[2,2,112,768]{3,2,1,0:T(8,128)(2,1)S(1)} %pad_maximum_fusion.1), channel_id=1, source_target_pairs={{0,4},{2,6},{4,0},{6,2},{8,12},{10,14},{12,8},{14,10},{16,20},{18,... | collective-permute-start | bytes 2064392 | tf_op jit(solution)/shard_map/ppermute | solution.py:44
  281.6 32.2 %copy-start.10 = (bf16[2,2,104,576]{3,2,1,0:T(8,128)(2,1)}, bf16[2,2,104,576]{3,2,1,0:T(8,128)(2,1)S(1)}, u32[]{:S(2)}) copy-start(bf16[2,2,104,576]{3,2,1,0:T(8,128)(2,1)S(1)} %copy.42) | copy-start | bytes 1437700
  281.6 26.3 %collective-permute-start.47 = (bf16[4,104,576]{2,1,0:T(8,128)(2,1)S(1)}, bf16[4,104,576]{2,1,0:T(8,128)(2,1)}, u32[]{:S(2)}, u32[]{:S(2)}) collective-permute-start(bf16[4,104,576]{2,1,0:T(8,128)(2,1)S(1)} %bitcast.79), channel_id=1, source_target_pairs={{0,4},{2,6},{4,0},{6,2},{8,12},{10,14},{12,8},{14,10},{16,20},{18,... | collective-permute-start | bytes 1437704 | tf_op jit(solution)/shard_map/ppermute | solution.py:44
  286.2 8.1 %collective-permute-start.48 = (bf16[384,256]{1,0:T(8,128)(2,1)S(1)}, bf16[384,256]{1,0:T(8,128)(2,1)}, u32[]{:S(2)}, u32[]{:S(2)}) collective-permute-start(bf16[384,256]{1,0:T(8,128)(2,1)S(1)} %get-tuple-element.329), channel_id=1, source_target_pairs={{0,8},{2,10},{4,12},{6,14},{8,0},{10,2},{12,4},{14,6},{16,24},{18,... | collective-permute-start | bytes 589832 | tf_op jit(solution)/shard_map/ppermute | solution.py:44
  288.5 18.8 %collective-permute-start.49 = (bf16[384,256]{1,0:T(8,128)(2,1)S(1)}, bf16[384,256]{1,0:T(8,128)(2,1)S(1)}, u32[]{:S(2)}, u32[]{:S(2)}) collective-permute-start(bf16[384,256]{1,0:T(8,128)(2,1)S(1)} %get-tuple-element.330), channel_id=1, source_target_pairs={{0,16},{2,18},{4,20},{6,22},{8,24},{10,26},{12,28},{14,30},{16,0},... | collective-permute-start | bytes 589832 | tf_op jit(solution)/shard_map/ppermute | solution.py:44
  288.5 18.8 %collective-permute-start.50 = (bf16[384,256]{1,0:T(8,128)(2,1)S(1)}, bf16[384,256]{1,0:T(8,128)(2,1)S(1)}, u32[]{:S(2)}, u32[]{:S(2)}) collective-permute-start(bf16[384,256]{1,0:T(8,128)(2,1)S(1)} %get-tuple-element.331), channel_id=1, source_target_pairs={{0,24},{2,26},{4,28},{6,30},{8,16},{10,18},{12,20},{14,22},{16,8},... | collective-permute-start | bytes 589832 | tf_op jit(solution)/shard_map/ppermute | solution.py:44
  294.4 16.3 %collective-permute-start.53 = (bf16[2,2,112,768]{3,2,1,0:T(8,128)(2,1)S(1)}, bf16[2,2,112,768]{3,2,1,0:T(8,128)(2,1)S(1)}, u32[]{:S(2)}, u32[]{:S(2)}) collective-permute-start(bf16[2,2,112,768]{3,2,1,0:T(8,128)(2,1)S(1)} %pad_maximum_fusion.1), channel_id=1, source_target_pairs={{0,2},{2,0},{4,6},{6,4},{8,10},{10,8},{12,14},{14,12},{16,18},{18,... | collective-permute-start | bytes 2064392 | tf_op jit(solution)/shard_map/ppermute | solution.py:44
  308.0 5.8 %collective-permute-start.54 = (bf16[2,2,112,768]{3,2,1,0:T(8,128)(2,1)S(1)}, bf16[2,2,112,768]{3,2,1,0:T(8,128)(2,1)S(1)}, u32[]{:S(2)}, u32[]{:S(2)}) collective-permute-start(bf16[2,2,112,768]{3,2,1,0:T(8,128)(2,1)S(1)} %collective-permute-done.46), channel_id=1, source_target_pairs={{0,2},{2,0},{4,6},{6,4},{8,10},{10,8},{12,14},{14,12},{16,18},{18,... | collective-permute-start | bytes 2064392 | tf_op jit(solution)/shard_map/ppermute | solution.py:44
  310.2 3.4 collective-permute-start.51
  310.3 3.5 %collective-permute-start.52 = (bf16[4,104,576]{2,1,0:T(8,128)(2,1)}, bf16[4,104,576]{2,1,0:T(8,128)(2,1)}, u32[]{:S(2)}, u32[]{:S(2)}) collective-permute-start(bf16[4,104,576]{2,1,0:T(8,128)(2,1)} %collective-permute-done.47.refs_6_), channel_id=1, source_target_pairs={{0,2},{2,0},{4,6},{6,4},{8,10},{10,8},{12,14},{14,12},{16,18},{18,... | collective-permute-start | bytes 1437704 | tf_op jit(solution)/shard_map/ppermute | solution.py:44
  (49 other events, 296.7 us)
Sparse Core Ops, SparseCore 0:
  204.6 37.5 reduce-scatter.1
  245.3 63.1 all-gather.2
